TPU v7x, 256 devices: a whole 4x4x8 slice. The times are simulated.
256 devices in a mesh: view: 64 (over z, y, core), feat: 4 (over x).
Axes of the slice: x: 4, y: 4, z: 8, core: 2. Of those that a mesh axis runs over, the one named last changes fastest.
Arguments:
- points: bfloat16 [4096, 768, 128], P('view', 'feat'), may hold values from -6 to 6
- head_weight: bfloat16 [768, 768], P('feat'), may hold values from -0.21875 to 0.21875
- teacher: bfloat16 [768, 128, 1369], P('feat', 'view'), may hold values from -6 to 6
- splat_weight: bfloat16 [128, 64, 74, 128], P('view'), may hold values from 0 to 0.19921875
- block_owner: int32 [128, 16, 4], P('view'), may hold values from 0 to 63, all different within a row; in each aligned block of 32 rows (0 to 31, 32 to 63, ..., all dimensions but the last counted through in order) at most 3 rows name the same one
- block_local: int32 [128, 64], P('view'), may hold values from 0 to 63
- block_row: int32 [128, 64], P('view'), may hold values from 0 to 35, as said below
Outputs:
- grad_points: bfloat16 [4096, 768, 128], P('view', 'feat')
- head_grad: float32 [768, 768], P('feat')
Inputs may be any that keep to these rules, and one draw needn't show every extreme that they name: `block_owner`: over the 128 list entries of the views of one index of view, no owner appears more than 3 times, and some owner appears exactly 3 times. `block_row`: each view's list holds every value from 0 to 35 at least once.
All inputs are finite; a program needn't handle non-finite values.
Results may differ from a plain program's by a relative error of at most 0.0064.
Values may be sent and summed in bfloat16 or wider, within the bound.
A program may use at most 128 MiB of HBM per device.

v0:
```python
import jax
import jax.numpy as jnp
from jax import lax
from jax.sharding import PartitionSpec as P

GRID = 37
BAND = 2
BLOCK = 128


def slot_plan(owners, peer_count, capacity):
    total_requests = owners.shape[0]
    positions = jnp.arange(total_requests, dtype=jnp.int32)
    earlier = (owners[:, None] == owners[None, :]) & (positions[None, :] < positions[:, None])
    slot_rank = jnp.sum(earlier.astype(jnp.int32), axis=1)
    target = owners * capacity + slot_rank
    slot_ids = jnp.arange(peer_count * capacity, dtype=jnp.int32)
    matches = target[None, :] == slot_ids[:, None]
    source = jnp.sum(jnp.where(matches, positions[None, :], 0), axis=1)
    filled = jnp.any(matches, axis=1)
    return (target, source, filled)


def per_device(points, head_weight, teacher, splat_weight, block_owner, block_local, block_row):
    peer_count = lax.axis_size("view")
    local_width = points.shape[1]
    view_count = splat_weight.shape[0]
    visible = splat_weight.shape[1]
    requests = view_count * visible
    capacity = max(3, (3 * requests + 2 * peer_count - 1) // (2 * peer_count))
    owners = block_owner.reshape(requests)
    local_ids = block_local.reshape(requests)
    target, source, filled = slot_plan(owners, peer_count, capacity)
    wanted = jnp.where(filled, jnp.take(local_ids, source), 0)
    columns = jnp.arange(GRID, dtype=jnp.int32)
    row_masks = [
        (block_row[:, :, None] + offset == columns[None, None, :]).astype(jnp.bfloat16)
        for offset in range(BAND)
    ]
    empty_bf = jnp.zeros((), jnp.bfloat16)
    asked_ids = lax.all_to_all(wanted, "view", split_axis=0, concat_axis=0, tiled=True)
    sent_rows = jnp.take(points, asked_ids, axis=0)
    arrived = lax.all_to_all(sent_rows, "view", split_axis=0, concat_axis=0, tiled=True)
    fetched = jnp.take(arrived, target, axis=0).reshape(view_count, visible, local_width, BLOCK)
    contrib = jnp.einsum(
        "vjcp,vjdp->vjcd", splat_weight, fetched, preferred_element_type=jnp.float32
    ).astype(jnp.bfloat16)
    rendered = jnp.zeros((view_count, GRID, GRID, local_width), jnp.float32)
    for offset in range(BAND):
        band_part = contrib[:, :, offset * GRID : (offset + 1) * GRID, :]
        rendered = rendered + jnp.einsum(
            "vjr,vjcd->vrcd", row_masks[offset], band_part, preferred_element_type=jnp.float32
        )
    rendered_rows = rendered.astype(jnp.bfloat16).reshape(view_count * GRID * GRID, local_width)
    pixel_rows = rendered_rows.shape[0]
    teacher_width = head_weight.shape[1]
    local_teacher = teacher.shape[0]
    contract_first = (((0,), (1,)), ((), ()))
    projected = lax.psum_scatter(
        lax.dot_general(
            head_weight, rendered_rows, contract_first, preferred_element_type=jnp.float32
        ),
        "feat",
        scatter_dimension=0,
        tiled=True,
    )
    square_sum = lax.psum(jnp.sum(projected * projected, axis=0), "feat")
    scale_rows = jnp.sqrt(square_sum / teacher_width + 1e-06)
    normed = projected / scale_rows[None, :]
    target_feat = teacher.reshape(local_teacher, pixel_rows).astype(jnp.float32)
    residual = normed - target_feat
    row_dot = lax.psum(jnp.sum(residual * normed, axis=0), "feat")
    grad_proj = (
        (residual - normed * (row_dot / teacher_width)[None, :]) / scale_rows[None, :]
    ).astype(jnp.bfloat16)
    shard_part = lax.all_gather(grad_proj, "feat", axis=0, tiled=True)
    grad_image = lax.dot_general(
        shard_part, head_weight, contract_first, preferred_element_type=jnp.float32
    )
    column_part = lax.dot_general(
        rendered_rows, shard_part, contract_first, preferred_element_type=jnp.float32
    )
    grad_head = column_part
    grad_image, grad_head = (grad_image, grad_head)
    head_grad = lax.psum(grad_head, "view") / (view_count * peer_count * GRID)
    grad_image = grad_image.astype(jnp.bfloat16).reshape(view_count, GRID, GRID, local_width)
    pieces = [
        jnp.einsum("vjr,vrcd->vjcd", row_mask, grad_image, preferred_element_type=jnp.float32)
        for row_mask in row_masks
    ]
    grad_contrib = jnp.concatenate(pieces, axis=2).astype(jnp.bfloat16)
    grad_block = jnp.einsum(
        "vjcp,vjcd->vjdp", splat_weight, grad_contrib, preferred_element_type=jnp.float32
    ).astype(jnp.bfloat16)
    grad_block = grad_block.reshape(requests, local_width, BLOCK)
    packed = jnp.where(filled[:, None, None], jnp.take(grad_block, source, axis=0), empty_bf)
    landed = lax.all_to_all(packed, "view", split_axis=0, concat_axis=0, tiled=True)
    summed = jax.ops.segment_sum(
        landed.astype(jnp.float32), asked_ids, num_segments=points.shape[0]
    )
    grad_points = summed.astype(jnp.bfloat16)
    return (grad_points, head_grad)


def solution(mesh):
    placed = (
        P("view", "feat", None),
        P("feat", None),
        P("feat", "view", None),
        P("view", None, None, None),
        P("view", None, None),
        P("view", None),
        P("view", None),
    )
    return jax.shard_map(
        per_device,
        mesh=mesh,
        in_specs=placed,
        out_specs=(P("view", "feat", None), P("feat", None)),
        check_vma=False,
    )
```

profile of v0, /device:TPU:2, one launch (start us, length us, event | category | flops | bytes accessed | tf_op | source)
XLA Modules:
  0.0 839.9 jit_solution(4426664382847408768)
XLA Ops:
  7.2 0.9 copy.41
  8.6 0.8 reshape.193
  9.7 1.6 gather_fusion
  11.4 21.5 %all_to_all.19 = s32[64,3,1]{1,2,0:T(1,128)S(1)} all-to-all(s32[64,3,1]{1,2,0:T(1,128)S(1)} %bitcast.40), channel_id=1, replica_groups=mesh['view'=64,'feat'=4] {'view'}, dimensions={0} | all-to-all | bytes 1536 | tf_op jit(solution)/shard_map/all_to_all | solution.py:41
  33.1 0.5 broadcast.172
  33.7 0.7 reduce.5
  34.6 9.6 %gather_fusion.1 = bf16[192,192,128]{2,1,0:T(8,128)(2,1)} fusion(bf16[64,192,128]{2,1,0:T(8,128)(2,1)S(1)} %copy-done, s32[1024]{0:T(1024)S(1)} %pad_clamp_fusion.1), kind=kCustom, calls=%fused_computation.1 | custom fusion | bytes 18875136 | tf_op jit(solution)/shard_map/jit(_take)/gather | solution.py:42
  44.1 8.2 broadcast_select_fusion
  52.4 5.9 all-to-all-start.1
  58.3 0.5 reduce-scatter.4.cloned.1.call-start
  59.2 207.7 %all-to-all-done.1 = bf16[192,192,128]{2,1,0:T(8,128)(2,1)} async-done(((bf16[192,192,128]{2,1,0:T(8,128)(2,1)}), bf16[192,192,128]{2,1,0:T(8,128)(2,1)}, u32[]{:S(2)}, u32[]{:S(2)}) %all-to-all-start.1) | async-done | bytes 9437216 | tf_op jit(solution)/shard_map/all_to_all | solution.py:43
  266.9 7.7 gather_fusion.2
  274.7 9.3 %convert_bitcast_fusion = bf16[2,64,74,192]{3,2,1,0:T(8,128)(2,1)} fusion(bf16[2,64,192,128]{3,2,1,0:T(8,128)(2,1)} %bitcast.38, pred[2,64]{1,0:T(4,128)(4,1)S(1)} %compare_and_fusion.1, bf16[2,64,74,128]{3,1,2,0:T(8,128)(2,1)S(1)} %copy-done.5), kind=kOutput, calls=%fused_computation.13 | convolution fusion | flops 470532096 | bytes 12353664 | tf_op jit(solution)/shard_map/vjcp,vjdp->vjcd/dot_general | solution.py:45
  284.0 4.3 fusion.36
  288.3 0.6 fusion.11
  288.9 0.7 add_convert_fusion
  289.6 0.3 copy.48
  289.9 0.7 reshape.194
  290.6 4.5 convolution_bitcast_fusion
  295.1 9.0 %copy.57 = f32[768,2738]{1,0:T(8,128)} copy(f32[768,2738]{0,1:T(8,128)} %convolution_bitcast_fusion) | data formatting | bytes 16822272
  304.3 1.2 copy-done.7
  305.4 1.7 reshape.197
  307.1 78.9 %reduce-scatter.4.cloned.1.call-done = f32[192,2738]{1,0:T(8,128)} async-done(((f32[768,2738]{1,0:T(8,128)}), f32[192,2738]{1,0:T(8,128)}) %reduce-scatter.4.cloned.1.call-update) | async-done | bytes 2102800 | tf_op jit(solution)/shard_map/reduce_scatter | solution.py:59
  386.1 3.4 copy.58
  389.4 2.2 multiply_reduce_fusion
  391.7 14.7 %psum.21 = f32[2738]{0:T(1024)S(1)} all-reduce(f32[2738]{0:T(1024)S(1)} %multiply_reduce_fusion), channel_id=1, replica_groups=mesh['view'=64,'feat'=4] {'feat'}, use_global_device_ids=true, to_apply=%region_5.6 | all-reduce | flops 2738 | bytes 21904 | tf_op jit(solution)/shard_map/psum | solution.py:67
  406.4 1.9 multiply_reduce_fusion.1
  408.3 15.2 %psum.22 = f32[2738]{0:T(1024)S(1)} all-reduce(f32[2738]{0:T(1024)S(1)} %multiply_reduce_fusion.1), channel_id=1, replica_groups=mesh['view'=64,'feat'=4] {'feat'}, use_global_device_ids=true, to_apply=%region_7.8 | all-reduce | flops 2738 | bytes 21904 | tf_op jit(solution)/shard_map/psum | solution.py:72
  423.5 3.0 divide_convert_fusion
  426.6 51.7 %all-gather.2.cloned.1.call-done = bf16[768,2738]{1,0:T(8,128)(2,1)} async-done(((bf16[192,2738]{1,0:T(8,128)(2,1)}), bf16[768,2738]{1,0:T(8,128)(2,1)}) %all-gather.2.cloned.1.call-update) | async-done | bytes 4205584 | tf_op jit(solution)/shard_map/all_gather | solution.py:76
  478.3 3.2 convolution_convert_fusion
  481.6 1.2 copy.50
  482.8 0.7 reshape.195
  483.5 0.8 convolution_convert_fusion.1
  484.3 0.8 convolution_convert_fusion.2
  485.2 0.8 pad_maximum_fusion
  486.0 0.9 copy-done.6
  486.9 7.4 fusion.5
  494.3 12.4 %gather_fusion.3 = bf16[192,192,128]{2,1,0:T(8,128)(2,1)} fusion(bf16[128,192,128]{2,1,0:T(8,128)(2,1)} %bitcast.37, s32[1024]{0:T(1024)S(1)} %pad_clamp_fusion.2), kind=kCustom, calls=%fused_computation.3 | custom fusion | bytes 18875136 | tf_op jit(solution)/shard_map/jit(_take)/gather | solution.py:96
  506.8 9.9 %select_select_fusion = bf16[192,192,128]{2,1,0:T(8,128)(2,1)} fusion(bf16[192,192,128]{2,1,0:T(8,128)(2,1)} %gather_fusion.3, pred[192]{0:T(512)(128)(4,1)S(1)} %compare_and_fusion.2, pred[192]{0:T(512)(128)(4,1)S(1)} %fusion.21), kind=kLoop, calls=%fused_computation.5 | loop fusion | flops 9437184 | bytes 18874752 | tf_op jit(solution)/shard_map/jit(_where)/select_n | solution.py:96
  516.6 10.8 %all-to-all-start.2 = ((bf16[192,192,128]{2,1,0:T(8,128)(2,1)}), bf16[192,192,128]{2,1,0:T(8,128)(2,1)}, u32[]{:S(2)}, u32[]{:S(2)}) async-start(bf16[192,192,128]{2,1,0:T(8,128)(2,1)} %select_select_fusion), calls=%async_computation.2 | async-start | bytes 18874368 | tf_op jit(solution)/shard_map/all_to_all | solution.py:97
  527.5 4.6 fusion.37
  532.2 232.3 %all-reduce.2.cloned.1.call-done = f32[192,768]{1,0:T(8,128)} async-done(((f32[192,768]{1,0:T(8,128)}), f32[192,768]{1,0:T(8,128)}) %all-reduce.2.cloned.1.call-update) | async-done | bytes 589840 | tf_op jit(solution)/shard_map/psum | solution.py:85
  764.5 1.9 broadcast_multiply_fusion
  766.5 12.4 %convert_element_type.45 = f32[192,192,128]{2,1,0:T(8,128)} convert(bf16[192,192,128]{2,1,0:T(8,128)(2,1)} %all-to-all-done.2) | non-fusion elementwise | flops 4718592 | bytes 28311552 | tf_op jit(solution)/shard_map/convert_element_type | solution.py:99
  778.9 3.4 broadcast_in_dim.79
  782.2 45.8 %scatter_fusion = f32[64,192,128]{2,1,0:T(8,128)} fusion(f32[64,192,128]{2,1,0:T(8,128)} %broadcast_in_dim.79, s32[192]{0:T(256)S(1)} %reshape.232, f32[192,192,128]{2,1,0:T(8,128)} %convert_element_type.45), kind=kCustom, calls=%fused_computation.4 | custom fusion | flops 4718592 | bytes 56623872 | tf_op jit(solution)/shard_map/scatter-add | solution.py:98
  828.1 5.0 convert_element_type.46
  (54 shorter events, 1.9 us)
Async XLA Ops:
  7.2 27.4 %copy-start = (bf16[64,192,128]{2,1,0:T(8,128)(2,1)S(1)}, bf16[64,192,128]{2,1,0:T(8,128)(2,1)}, u32[]{:S(2)}) copy-start(bf16[64,192,128]{2,1,0:T(8,128)(2,1)} %param.7) | copy-start | bytes 9437188
  52.4 6.4 copy-start.9
  52.4 6.8 copy-start.10
  52.4 214.5 %all-to-all-start.1 = ((bf16[192,192,128]{2,1,0:T(8,128)(2,1)}), bf16[192,192,128]{2,1,0:T(8,128)(2,1)}, u32[]{:S(2)}, u32[]{:S(2)}) async-start(bf16[192,192,128]{2,1,0:T(8,128)(2,1)} %broadcast_select_fusion), calls=%async_computation.1 | async-start | bytes 18874368 | tf_op jit(solution)/shard_map/all_to_all | solution.py:43
  58.3 327.8 %reduce-scatter.4.cloned.1.call-start = ((), (), s32[]{:S(2)}) async-start(), calls=%async_computation.6 | async-start | bytes 10813440 | tf_op jit(solution)/shard_map/reduce_scatter | solution.py:59
  59.2 215.4 %copy-start.5 = (bf16[2,64,74,128]{3,1,2,0:T(8,128)(2,1)S(1)}, bf16[2,64,74,128]{3,1,2,0:T(8,128)(2,1)}, u32[]{:S(2)}) copy-start(bf16[2,64,74,128]{3,1,2,0:T(8,128)(2,1)} %param.10) | copy-start | bytes 7274500
  289.5 1.0 copy-start.8
  290.6 4.5 copy-start.3
  304.2 1.2 copy-start.7
  304.2 174.1 %all-gather.2.cloned.1.call-start = ((), (), s32[]{:S(2)}) async-start(), calls=%async_computation.4 | async-start | bytes 5406720 | tf_op jit(solution)/shard_map/all_gather | solution.py:76
  386.0 20.3 %copy-start.2 = (f32[192,2738]{1,0:T(8,128)S(1)}, f32[192,2738]{1,0:T(8,128)}, u32[]{:S(2)}) copy-start(f32[192,2738]{1,0:T(8,128)} %reduce-scatter.4.cloned.1.call-done) | copy-start | bytes 6308356
  485.2 1.7 copy-start.6
  516.6 10.9 %copy-start.4 = (bf16[2738,192]{1,0:T(8,128)(2,1)S(1)}, bf16[2738,192]{1,0:T(8,128)(2,1)}, u32[]{:S(2)}) copy-start(bf16[2738,192]{1,0:T(8,128)(2,1)} %copy-done.3) | copy-start | bytes 3154180
  516.6 249.8 %all-to-all-start.2 = ((bf16[192,192,128]{2,1,0:T(8,128)(2,1)}), bf16[192,192,128]{2,1,0:T(8,128)(2,1)}, u32[]{:S(2)}, u32[]{:S(2)}) async-start(bf16[192,192,128]{2,1,0:T(8,128)(2,1)} %select_select_fusion), calls=%async_computation.2 | async-start | bytes 18874368 | tf_op jit(solution)/shard_map/all_to_all | solution.py:97
  527.5 237.1 %all-reduce.2.cloned.1.call-start = ((), (), s32[]{:S(2)}) async-start(), calls=%async_computation.5 | async-start | bytes 1179648 | tf_op jit(solution)/shard_map/psum | solution.py:85
  782.2 50.9 %copy-start.1 = (bf16[64,192,128]{2,1,0:T(8,128)(2,1)S(1)}, bf16[64,192,128]{2,1,0:T(8,128)(2,1)}, u32[]{:S(2)}) copy-start(bf16[64,192,128]{2,1,0:T(8,128)(2,1)} %param.7) | copy-start | bytes 9437188
Sparse Core Ops, SparseCore 0:
  304.3 81.6 reduce-scatter.3
  426.7 51.5 all-gather.1
  532.3 232.1 all-reduce.1
where the time goes:
time: 852 us; the launch traced here: 840 us
  waiting for transfers between devices  571 us (67%)
  other arithmetic  92.5 us (11%)
  local copies, waits for them, and re-layouts  61.5 us (7%)
  blocking collectives  51.5 us (6%)
  matrix products  32.1 us (4%)
  starting transfers between devices  17.3 us (2%)
  between operations  14.3 us (2%)
    psum x1, waiting for transfers between devices, per_device(): head_grad = lax.psum(grad_head, 'view') / (view_count * peer_count * GRID)  232 us
    all_to_all x1, waiting for transfers between devices, per_device(): lax.all_to_all(sent_rows, 'view', split_axis=0, concat_axis=0, tiled=True)  208 us
    reduce_scatter x1, waiting for transfers between devices, per_device(): lax.psum_scatter(lax.dot_general(head_weight, rendered_rows, contract_fir...  78.9 us
    all_gather x1, waiting for transfers between devices, per_device(): shard_part = lax.all_gather(grad_proj, 'feat', axis=0, tiled=True)  51.7 us
    scatter-add x1, other arithmetic, per_device(): jax.ops.segment_sum(landed.astype(jnp.float32), asked_ids, num_segments=p...  45.8 us
    all_to_all x1, blocking collectives, per_device(): lax.all_to_all(wanted, 'view', split_axis=0, concat_axis=0, tiled=True)  21.5 us
  transfers between devices with their start and end apart: 5, of which 4 were waited for; matrix products, arithmetic and copies ran while one was open for 1% of the time, Pallas kernels for 0%

commit v1 on v0

v1 whole, which is shorter than its diff:
```python
import functools

import jax
import jax.numpy as jnp
from jax import lax
from jax.experimental import pallas as pl
from jax.experimental.pallas import tpu as pltpu
from jax.sharding import PartitionSpec as P

GRID = 37
BAND = 2
BLOCK = 128
CAP = 3
ROWS = BAND * GRID
PIECE = 24
SLOT = 112
LINE = 40
STEP = 8
SMEM = functools.partial(pl.BlockSpec, memory_space=pltpu.SMEM)
NT = (((1,), (1,)), ((), ()))
TN = (((0,), (0,)), ((), ()))
VMEM_LIMIT = 60 * 1024 * 1024


def params(**kw):
    return pltpu.CompilerParams(vmem_limit_bytes=VMEM_LIMIT, **kw)


def slot_plan(owners, peer_count, capacity):
    total_requests = owners.shape[0]
    positions = jnp.arange(total_requests, dtype=jnp.int32)
    earlier = (owners[:, None] == owners[None, :]) & (positions[None, :] < positions[:, None])
    slot_rank = jnp.sum(earlier.astype(jnp.int32), axis=1)
    target = owners * capacity + slot_rank
    slot_ids = jnp.arange(peer_count * capacity, dtype=jnp.int32)
    matches = target[None, :] == slot_ids[:, None]
    source = jnp.sum(jnp.where(matches, positions[None, :], 0), axis=1)
    filled = jnp.any(matches, axis=1)
    return source, filled.astype(jnp.int32)


def pack_weights_kernel(source, filled, local, last, weights, out):
    step = pl.program_id(0)
    row = lax.broadcasted_iota(jnp.int32, (PIECE, BLOCK), 0)

    def one(i, carry):
        for s in range(CAP):
            t = (step * STEP + i) * CAP + s
            src = source[t]
            piece = weights[src].astype(jnp.float32)
            piece = jnp.where(filled[t] > 0, piece, 0.0)
            tag = local[src].astype(jnp.float32)
            piece = jnp.where((row == PIECE - 1) & (last[0] > 0), tag, piece)
            out[i, pl.ds(s * PIECE, PIECE), :] = piece.astype(jnp.bfloat16)
        return carry

    lax.fori_loop(0, STEP, one, 0)


def pack_weights(source, filled, local, last, weights, peers):
    return pl.pallas_call(
        pack_weights_kernel,
        out_shape=jax.ShapeDtypeStruct((peers, CAP * PIECE, BLOCK), jnp.bfloat16),
        grid=(peers // STEP,),
        in_specs=[SMEM(), SMEM(), SMEM(), SMEM(), pl.BlockSpec(weights.shape, lambda i: (0, 0, 0))],
        out_specs=pl.BlockSpec((STEP, CAP * PIECE, BLOCK), lambda i: (i, 0, 0)),
        compiler_params=params(),
        name="pack_weights",
    )(source, filled, local, last, weights)


def slot_weights(pieces, i, s):
    base = s * PIECE
    parts = [pieces[f, i, pl.ds(base, PIECE), :] for f in range(3)]
    parts.append(pieces[3, i, pl.ds(base, 8), :])
    return jnp.concatenate([p.astype(jnp.float32) for p in parts], axis=0).astype(jnp.bfloat16)


def splat_kernel(ids, points, pieces, out, buf):
    step = pl.program_id(0)
    lane = lax.broadcasted_iota(jnp.int32, (GRID, BLOCK), 1)

    def one(i, carry):
        for s in range(CAP):
            block = points[ids[(step * STEP + i) * CAP + s]]
            wide = jnp.concatenate([block, block[128:192]], axis=0)
            product = lax.dot_general(slot_weights(pieces, i, s), wide, NT, preferred_element_type=jnp.float32)
            rest = product[:, 128:256]
            buf[s, 0:80, :] = product[:, 0:128]
            buf[s, ROWS : ROWS + GRID, :] = jnp.where(lane < 64, rest[0:GRID], rest[GRID:ROWS])
            buf[s, SLOT - 1 : SLOT, :] = jnp.zeros((1, BLOCK), jnp.float32)
            out[i, pl.ds(s * SLOT, SLOT), :] = buf[s].astype(jnp.bfloat16)
        return carry

    lax.fori_loop(0, STEP, one, 0)


def splat(ids, points, pieces):
    peers = pieces.shape[1]
    return pl.pallas_call(
        splat_kernel,
        out_shape=jax.ShapeDtypeStruct((peers, CAP * SLOT, BLOCK), jnp.bfloat16),
        grid=(peers // STEP,),
        in_specs=[
            SMEM(),
            pl.BlockSpec(points.shape, lambda i: (0, 0, 0)),
            pl.BlockSpec((4, STEP, CAP * PIECE, BLOCK), lambda i: (0, i, 0, 0)),
        ],
        out_specs=pl.BlockSpec((STEP, CAP * SLOT, BLOCK), lambda i: (i, 0, 0)),
        scratch_shapes=[pltpu.VMEM((CAP, SLOT, BLOCK), jnp.float32)],
        compiler_params=params(),
        name="splat",
    )(ids, points, pieces)


def render_kernel(lines, source, line_of, arrived, out, acc):
    step = pl.program_id(0)

    @pl.when(step == 0)
    def _():
        acc[...] = jnp.zeros_like(acc)

    def one(i, carry):
        for s in range(CAP):
            at = line_of[source[(step * STEP + i) * CAP + s]] + 1
            acc[at] += arrived[i, pl.ds(s * SLOT, SLOT), :].astype(jnp.float32)
        return carry

    lax.fori_loop(0, STEP, one, 0)

    @pl.when(step == pl.num_programs(0) - 1)
    def _():
        def finish(k, carry):
            upper, own = acc[k], acc[k + 1]
            main = own[0:GRID] + upper[GRID:ROWS]
            pair = own[ROWS : ROWS + GRID] + pltpu.roll(upper, 64, 1)[ROWS : ROWS + GRID]
            out[k, 0:GRID, 0:128] = main.astype(jnp.bfloat16)
            out[k, 0:GRID, 128:192] = pair[:, 0:64].astype(jnp.bfloat16)
            return carry

        out[...] = jnp.zeros_like(out)
        lax.fori_loop(0, lines, finish, 0)


def render(source, line_of, arrived, lines, padded):
    peers = arrived.shape[0]
    return pl.pallas_call(
        functools.partial(render_kernel, lines),
        out_shape=jax.ShapeDtypeStruct((padded, LINE, 192), jnp.bfloat16),
        grid=(peers // STEP,),
        in_specs=[SMEM(), SMEM(), pl.BlockSpec((STEP, CAP * SLOT, BLOCK), lambda i: (i, 0, 0))],
        out_specs=pl.BlockSpec((padded, LINE, 192), lambda i: (0, 0, 0)),
        scratch_shapes=[pltpu.VMEM((lines + 1, SLOT, BLOCK), jnp.float32)],
        compiler_params=params(),
        name="render",
    )(source, line_of, arrived)


def compare_kernel(rendered, head, target, grad_image, grad_proj):
    width = target.shape[1]
    projected = jnp.zeros(target.shape, jnp.float32)
    for f in range(4):
        projected += jnp.dot(rendered[f], head[f], preferred_element_type=jnp.float32)
    scale = jnp.sqrt(jnp.sum(projected * projected, axis=1, keepdims=True) / width + 1e-06)
    inverse = 1.0 / scale
    normed = projected * inverse
    residual = normed - target[...].astype(jnp.float32)
    row_dot = jnp.sum(residual * normed, axis=1, keepdims=True) / width
    grad = ((residual - normed * row_dot) * inverse).astype(jnp.bfloat16)
    grad_proj[...] = grad
    for f in range(4):
        grad_image[f] = lax.dot_general(grad, head[f], NT, preferred_element_type=jnp.float32).astype(jnp.bfloat16)


def compare(rendered, head, target):
    rows, width = target.shape
    part = rows // 5
    return pl.pallas_call(
        compare_kernel,
        out_shape=(
            jax.ShapeDtypeStruct(rendered.shape, jnp.bfloat16),
            jax.ShapeDtypeStruct(target.shape, jnp.bfloat16),
        ),
        grid=(5,),
        in_specs=[
            pl.BlockSpec((4, part, 192), lambda i: (0, i, 0)),
            pl.BlockSpec(head.shape, lambda i: (0, 0, 0)),
            pl.BlockSpec((part, width), lambda i: (i, 0)),
        ],
        out_specs=(
            pl.BlockSpec((4, part, 192), lambda i: (0, i, 0)),
            pl.BlockSpec((part, width), lambda i: (i, 0)),
        ),
        compiler_params=params(),
        name="compare",
    )(rendered, head, target)


def pack_grads_kernel(lines, source, line_of, image, out, slots, buf):
    step = pl.program_id(0)

    @pl.when(step == 0)
    def _():
        def build(k, carry):
            own, lower = image[k].astype(jnp.float32), image[k + 1].astype(jnp.float32)
            buf[0:GRID, :] = own[0:GRID, 0:128]
            buf[GRID:ROWS, :] = lower[0:GRID, 0:128]
            pair = jnp.concatenate([own[0:GRID, 128:192], lower[0:GRID, 128:192]], axis=1)
            buf[ROWS : ROWS + GRID, :] = pair
            slots[k] = buf[...].astype(jnp.bfloat16)
            return carry

        buf[...] = jnp.zeros_like(buf)
        lax.fori_loop(0, lines, build, 0)

    def one(i, carry):
        for s in range(CAP):
            out[i, pl.ds(s * SLOT, SLOT), :] = slots[line_of[source[(step * STEP + i) * CAP + s]]]
        return carry

    lax.fori_loop(0, STEP, one, 0)


def pack_grads(source, line_of, image, peers, lines):
    return pl.pallas_call(
        functools.partial(pack_grads_kernel, lines),
        out_shape=jax.ShapeDtypeStruct((peers, CAP * SLOT, BLOCK), jnp.bfloat16),
        grid=(peers // STEP,),
        in_specs=[SMEM(), SMEM(), pl.BlockSpec(image.shape, lambda i: (0, 0, 0))],
        out_specs=pl.BlockSpec((STEP, CAP * SLOT, BLOCK), lambda i: (i, 0, 0)),
        scratch_shapes=[
            pltpu.VMEM((lines, SLOT, BLOCK), jnp.bfloat16),
            pltpu.VMEM((SLOT, BLOCK), jnp.float32),
        ],
        compiler_params=params(),
        name="pack_grads",
    )(source, line_of, image)


def unsplat_kernel(ids, pieces, arrived, out, acc):
    step = pl.program_id(0)
    lane = lax.broadcasted_iota(jnp.int32, (GRID, BLOCK), 1)

    @pl.when(step == 0)
    def _():
        acc[...] = jnp.zeros_like(acc)

    def one(i, carry):
        for s in range(CAP):
            at = ids[(step * STEP + i) * CAP + s]
            weights = slot_weights(pieces, i, s)
            slot = arrived[i, pl.ds(s * SLOT, SLOT), :].astype(jnp.float32)
            pair = slot[ROWS : ROWS + GRID]
            rest = jnp.concatenate(
                [jnp.where(lane < 64, pair, 0.0), jnp.where(lane < 64, 0.0, pair), jnp.zeros((6, BLOCK), jnp.float32)], axis=0
            )
            both = jnp.concatenate([slot[0:80], rest], axis=1).astype(jnp.bfloat16)
            product = lax.dot_general(both, weights, TN, preferred_element_type=jnp.float32)
            acc[at, 0:128, :] += product[0:128].astype(jnp.bfloat16).astype(jnp.float32)
            acc[at, 128:192, :] += (product[128:192] + product[192:256]).astype(jnp.bfloat16).astype(jnp.float32)
        return carry

    lax.fori_loop(0, STEP, one, 0)

    @pl.when(step == pl.num_programs(0) - 1)
    def _():
        out[...] = acc[...].astype(jnp.bfloat16)


def unsplat(ids, pieces, arrived, shape):
    peers = arrived.shape[0]
    return pl.pallas_call(
        unsplat_kernel,
        out_shape=jax.ShapeDtypeStruct(shape, jnp.bfloat16),
        grid=(peers // STEP,),
        in_specs=[
            SMEM(),
            pl.BlockSpec((4, STEP, CAP * PIECE, BLOCK), lambda i: (0, i, 0, 0)),
            pl.BlockSpec((STEP, CAP * SLOT, BLOCK), lambda i: (i, 0, 0)),
        ],
        out_specs=pl.BlockSpec(shape, lambda i: (0, 0, 0)),
        scratch_shapes=[pltpu.VMEM(shape, jnp.float32)],
        compiler_params=params(),
        name="unsplat",
    )(ids, pieces, arrived)


def per_device(points, head_weight, teacher, splat_weight, block_owner, block_local, block_row):
    peers = lax.axis_size("view")
    feat = lax.axis_index("feat")
    local_width = points.shape[1]
    views, visible = splat_weight.shape[:2]
    requests = views * visible
    lines = views * GRID
    share = -(-lines // 4)
    padded = 4 * share
    rows = share * LINE

    source, filled = slot_plan(block_owner.reshape(requests), peers, CAP)
    local = block_local.reshape(requests)
    line_of = (block_row + jnp.arange(views, dtype=jnp.int32)[:, None] * GRID).reshape(requests)
    last = (feat == 3).astype(jnp.int32).reshape(1)

    mine = lax.dynamic_slice_in_dim(
        jnp.pad(splat_weight, ((0, 0), (0, 0), (0, 4 * PIECE - ROWS), (0, 0))), feat * PIECE, PIECE, axis=2
    ).reshape(requests, PIECE, BLOCK)
    packed = pack_weights(source, filled, local, last, mine, peers)
    swapped = lax.all_to_all(packed, "view", split_axis=0, concat_axis=0, tiled=True)
    pieces = lax.all_gather(swapped, "feat", axis=0)
    ids = pieces[3].reshape(peers, CAP, PIECE, BLOCK)[:, :, PIECE - 1, 0].astype(jnp.int32).reshape(peers * CAP)

    head = lax.all_gather(head_weight, "feat", axis=0)
    wanted = jnp.pad(
        teacher.reshape(local_width, lines, GRID), ((0, 0), (0, padded - lines), (0, LINE - GRID))
    ).reshape(local_width, 4, rows)
    target = lax.all_to_all(wanted.transpose(1, 0, 2), "feat", split_axis=0, concat_axis=0, tiled=True)
    target = target.reshape(4 * local_width, rows).T

    contrib = splat(ids, points, pieces)
    arrived = lax.all_to_all(contrib, "view", split_axis=0, concat_axis=0, tiled=True)
    image = render(source, line_of, arrived, lines, padded).reshape(4, rows, local_width)
    rendered = lax.all_to_all(image, "feat", split_axis=0, concat_axis=0, tiled=True)
    grad_image, grad_proj = compare(rendered, head, target)
    grad_rows = lax.all_to_all(grad_image, "feat", split_axis=0, concat_axis=0, tiled=True)
    grads = pack_grads(source, line_of, grad_rows.reshape(padded, LINE, local_width), peers, lines)
    landed = lax.all_to_all(grads, "view", split_axis=0, concat_axis=0, tiled=True)
    grad_points = unsplat(ids, pieces, landed, points.shape)

    head_part = jnp.einsum("frd,rt->fdt", rendered, grad_proj, preferred_element_type=jnp.float32)
    head_part = lax.psum_scatter(head_part, "feat", scatter_dimension=0, tiled=False)
    head_grad = lax.psum(head_part, "view") / (views * peers * GRID)
    return grad_points, head_grad


def solution(mesh):
    placed = (
        P("view", "feat", None),
        P("feat", None),
        P("feat", "view", None),
        P("view", None, None, None),
        P("view", None, None),
        P("view", None),
        P("view", None),
    )
    return jax.shard_map(
        per_device,
        mesh=mesh,
        in_specs=placed,
        out_specs=(P("view", "feat", None), P("feat", None)),
        check_vma=False,
    )
```

time: 852 us -> 628 us (0.74); the launches traced: 840 us -> 627 us
  waiting for transfers between devices: 571 us -> 420 us
  other arithmetic: 92.5 us -> 3.59 us
  Pallas kernels: 0 us -> 75.4 us
  local copies, waits for them, and re-layouts: 61.5 us -> 20.3 us
  matrix products: 32.1 us -> 2.49 us
  starting transfers between devices: 17.3 us -> 31.8 us
    all_to_all x2 -> x4, waiting for transfers between devices: 208 us -> 131 us  [the longest x1 119 us: per_device(): lax.all_to_all(contrib, 'view', split_axis=0, concat_axis=0, tiled=True)]
    pallas_call x0 -> x6, Pallas kernels: none -> 75.4 us  [the longest x1 20.3 us: unsplat(): pl.pallas_call(unsplat_kernel, out_shape=jax.ShapeDtypeStruct(shape, jnp....]
    scatter-add x1 -> x0, other arithmetic: 45.8 us -> none  [per_device(): jax.ops.segment_sum(landed.astype(jnp.float32), asked_ids, num_segments=p...]
    reduce_scatter x1, waiting for transfers between devices: 78.9 us -> 34.6 us  [per_device(): lax.psum_scatter(head_part, 'feat', scatter_dimension=0, tiled=False)]
    all_to_all x1 -> x2, blocking collectives: 21.5 us -> 59.3 us  [the longest x1 43.9 us: per_device(): lax.all_to_all(packed, 'view', split_axis=0, concat_axis=0, tiled=True)]
    gather x5 -> x0, local copies, waits for them, and re-layouts: 31.4 us -> none  [the longest x1 12.4 us: per_device(): jnp.take(grad_block, source, axis=0)]
    psum x2 -> x0, blocking collectives: 29.9 us -> none  [the longest x1 15.2 us: per_device(): row_dot = lax.psum(jnp.sum(residual * normed, axis=0), 'feat')]
    dot_general x9 -> x1, matrix products: 32.1 us -> 2.49 us  [per_device(): jnp.einsum('frd,rt->fdt', rendered, grad_proj, preferred_element_type=jnp...]
  transfers between devices with their start and end apart: 5 -> 8, of which waited for: 4 -> 5; matrix products, arithmetic and copies ran while one was open for 1% -> 2% of each run, Pallas kernels for 0% -> 2%
where the time goes in v1:
time: 628 us; the launch traced here: 627 us
  waiting for transfers between devices  420 us (67%)
  Pallas kernels  75.4 us (12%)
  blocking collectives  59.3 us (9%)
  starting transfers between devices  31.8 us (5%)
  local copies, waits for them, and re-layouts  20.3 us (3%)
  between operations  13.9 us (2%)
    psum x1, waiting for transfers between devices, per_device(): head_grad = lax.psum(head_part, 'view') / (views * peers * GRID)  203 us
    all_to_all x1, waiting for transfers between devices, per_device(): lax.all_to_all(contrib, 'view', split_axis=0, concat_axis=0, tiled=True)  119 us
    all_gather x1, waiting for transfers between devices, per_device(): pieces = lax.all_gather(swapped, 'feat', axis=0)  51.1 us
    all_to_all x1, blocking collectives, per_device(): lax.all_to_all(packed, 'view', split_axis=0, concat_axis=0, tiled=True)  43.9 us
    reduce_scatter x1, waiting for transfers between devices, per_device(): lax.psum_scatter(head_part, 'feat', scatter_dimension=0, tiled=False)  34.6 us
    pallas_call x1, Pallas kernels, unsplat(): pl.pallas_call(unsplat_kernel, out_shape=jax.ShapeDtypeStruct(shape, jnp....  20.3 us
    pallas_call x1, Pallas kernels, splat(): pl.pallas_call(splat_kernel, out_shape=jax.ShapeDtypeStruct((peers, CAP *...  17.2 us
    all_to_all x1, blocking collectives, per_device(): lax.all_to_all(grad_image, 'feat', split_axis=0, concat_axis=0, tiled=True)  15.4 us
  transfers between devices with their start and end apart: 8, of which 5 were waited for; matrix products, arithmetic and copies ran while one was open for 2% of the time, Pallas kernels for 2%

profile of v1, /device:TPU:2, one launch (start us, length us, event | category | flops | bytes accessed | tf_op | source)
XLA Modules:
  0.0 627.2 jit_solution(12241662858531833686)
XLA Ops:
  7.2 0.0 all-gather.5.cloned.1.call-start
  7.2 0.8 copy.29
  8.0 0.1 reshape.55
  8.1 0.2 convert_reduce_fusion
  8.3 0.7 select_reduce_fusion.source
  9.0 0.1 fusion.2
  9.1 1.4 pad_dynamic-slice_fusion
  10.5 1.4 copy.30
  11.9 0.6 convert_element_type.19.filled
  12.4 0.6 reshape.56.local
  13.0 4.5 pack_weights.1
  17.6 43.9 %all_to_all.30 = bf16[64,72,128]{2,1,0:T(8,128)(2,1)} all-to-all(bf16[64,72,128]{2,1,0:T(8,128)(2,1)} %pack_weights.1), channel_id=1, replica_groups=mesh['view'=64,'feat'=4] {'view'}, dimensions={0} | all-to-all | bytes 2359296 | tf_op jit(solution)/shard_map/all_to_all | solution.py:308
  61.5 51.1 %all-gather.5.cloned.1.call-done = bf16[256,72,128]{2,1,0:T(8,128)(2,1)} async-done(((bf16[64,72,128]{2,1,0:T(8,128)(2,1)}), bf16[256,72,128]{2,1,0:T(8,128)(2,1)}) %all-gather.5.cloned.1.call-update) | async-done | bytes 4718608 | tf_op jit(solution)/shard_map/all_gather | solution.py:309
  112.6 1.3 slice-done
  113.8 0.1 slice.10
  113.9 0.5 copy.39
  114.4 0.7 reshape.68.ids
  115.2 17.2 %splat.1 = bf16[64,336,128]{2,1,0:T(8,128)(2,1)} custom-call(s32[192]{0:T(256)} %reshape.68.ids, bf16[64,192,128]{2,1,0:T(8,128)(2,1)} %points.1, bf16[4,64,72,128]{3,2,1,0:T(8,128)(2,1)} %bitcast.23), custom_call_target="tpu_custom_call" | custom-call | tf_op jit(solution)/shard_map/splat/pallas_call | solution.py:100
  132.4 10.8 %all-to-all-start.1 = ((bf16[64,336,128]{2,1,0:T(8,128)(2,1)}), bf16[64,336,128]{2,1,0:T(8,128)(2,1)}, u32[]{:S(2)}, u32[]{:S(2)}) async-start(bf16[64,336,128]{2,1,0:T(8,128)(2,1)} %splat.1), calls=%async_computation.1 | async-start | bytes 11010048 | tf_op jit(solution)/shard_map/all_to_all | solution.py:320
  143.2 0.0 all-gather.7.cloned.1.call-start
  143.3 0.7 all-gather.7.cloned.1.call-update
  144.0 1.8 copy.33
  145.8 0.7 reshape.62
  146.5 0.3 pad.9
  146.8 1.5 copy.34
  148.3 119.4 %all-to-all-done.1.arrived = bf16[64,336,128]{2,1,0:T(8,128)(2,1)} async-done(((bf16[64,336,128]{2,1,0:T(8,128)(2,1)}), bf16[64,336,128]{2,1,0:T(8,128)(2,1)}, u32[]{:S(2)}, u32[]{:S(2)}) %all-to-all-start.1) | async-done | bytes 5505056 | tf_op jit(solution)/shard_map/all_to_all | solution.py:320
  267.6 4.6 all-to-all-start.3
  272.2 0.1 broadcast_add_fusion
  272.3 0.6 reshape.60.line_of
  272.9 13.2 %render.1 = bf16[76,40,192]{2,1,0:T(8,128)(2,1)} custom-call(s32[192]{0:T(256)} %select_reduce_fusion.source, s32[128]{0:T(128)} %reshape.60.line_of, bf16[64,336,128]{2,1,0:T(8,128)(2,1)} %all-to-all-done.1.arrived), custom_call_target="tpu_custom_call" | custom-call | tf_op jit(solution)/shard_map/render/pallas_call | solution.py:147
  286.0 2.5 copy.32
  288.5 4.8 all-to-all-start.2
  293.3 1.4 copy.35
  294.7 11.3 %all-to-all-done.2 = bf16[4,760,192]{1,2,0:T(8,128)(2,1)S(1)} async-done(((bf16[4,760,192]{1,2,0:T(8,128)(2,1)}), bf16[4,760,192]{1,2,0:T(8,128)(2,1)S(1)}, u32[]{:S(2)}, u32[]{:S(2)}) %all-to-all-start.2) | async-done | bytes 1167392 | tf_op jit(solution)/shard_map/all_to_all | solution.py:322
  306.0 1.5 copy.36.rendered
  307.5 8.5 %compare.3 = (bf16[4,760,192]{2,1,0:T(8,128)(2,1)}, bf16[760,768]{1,0:T(8,128)(2,1)}) custom-call(bf16[4,760,192]{2,1,0:T(8,128)(2,1)} %copy.36.rendered, bf16[4,192,768]{2,1,0:T(8,128)(2,1)} %bitcast.32, bf16[760,768]{1,0:T(8,128)(2,1)} %bitcast.30), custom_call_target="tpu_custom_call" | custom-call | tf_op jit(solution)/shard_map/compare/pallas_call | solution.py:178
  316.1 1.7 copy.37
  317.7 15.4 %all_to_all.31 = bf16[4,760,192]{1,2,0:T(8,128)(2,1)S(1)} all-to-all(bf16[4,760,192]{1,2,0:T(8,128)(2,1)S(1)} %copy.37), channel_id=1, replica_groups=mesh['view'=64,'feat'=4] {'feat'}, dimensions={0} | all-to-all | bytes 2334720 | tf_op jit(solution)/shard_map/all_to_all | solution.py:324
  333.2 1.5 copy.38
  334.7 11.7 %pack_grads.1 = bf16[64,336,128]{2,1,0:T(8,128)(2,1)} custom-call(s32[192]{0:T(256)} %select_reduce_fusion.source, s32[128]{0:T(128)} %reshape.60.line_of, bf16[76,40,192]{2,1,0:T(8,128)(2,1)} %bitcast.27), custom_call_target="tpu_custom_call" | custom-call | tf_op jit(solution)/shard_map/pack_grads/pallas_call | solution.py:225
  346.4 11.4 %all-to-all-start.5 = ((bf16[64,336,128]{2,1,0:T(8,128)(2,1)}), bf16[64,336,128]{2,1,0:T(8,128)(2,1)}, u32[]{:S(2)}, u32[]{:S(2)}) async-start(bf16[64,336,128]{2,1,0:T(8,128)(2,1)} %pack_grads.1), calls=%async_computation.5 | async-start | bytes 11010048 | tf_op jit(solution)/shard_map/all_to_all | solution.py:326
  357.9 0.0 reduce-scatter.2.cloned.1.call-start
  357.9 2.5 fusion
  360.4 0.0 all-reduce.4.cloned.1.call-start
  360.5 34.6 %reduce-scatter.2.cloned.1.call-done = f32[1,192,768]{2,1,0:T(8,128)} async-done(((f32[4,192,768]{2,1,0:T(8,128)}), f32[1,192,768]{2,1,0:T(8,128)}) %reduce-scatter.2.cloned.1.call-update) | async-done | bytes 589840 | tf_op jit(solution)/shard_map/reduce_scatter | solution.py:330
  395.1 203.3 %all-reduce.4.cloned.1.call-done = f32[192,768]{1,0:T(8,128)} async-done(((f32[192,768]{1,0:T(8,128)}), f32[192,768]{1,0:T(8,128)}) %all-reduce.4.cloned.1.call-update) | async-done | bytes 589840 | tf_op jit(solution)/shard_map/psum | solution.py:331
  598.4 1.9 broadcast_multiply_fusion
  600.4 20.3 %unsplat.1 = bf16[64,192,128]{2,1,0:T(8,128)(2,1)} custom-call(s32[192]{0:T(256)} %reshape.68.ids, bf16[4,64,72,128]{3,2,1,0:T(8,128)(2,1)} %bitcast.24, bf16[64,336,128]{2,1,0:T(8,128)(2,1)} %all-to-all-done.5.arrived), custom_call_target="tpu_custom_call" | custom-call | tf_op jit(solution)/shard_map/unsplat/pallas_call | solution.py:272
  (18 shorter events, 0.1 us)
Async XLA Ops:
  7.2 105.4 %all-gather.5.cloned.1.call-start = ((), (), s32[]{:S(2)}) async-start(), calls=%async_computation.9 | async-start | bytes 5898240 | tf_op jit(solution)/shard_map/all_gather | solution.py:309
  10.4 2.0 copy-start.3
  112.6 1.3 slice-start
  132.4 11.6 %copy-start = (bf16[192,2,1369]{2,1,0:T(2,128)(2,1)S(1)}, bf16[192,2,1369]{2,1,0:T(2,128)(2,1)}, u32[]{:S(2)}) copy-start(bf16[192,2,1369]{2,1,0:T(2,128)(2,1)} %param.9) | copy-start | bytes 3154180
  132.4 135.3 %all-to-all-start.1 = ((bf16[64,336,128]{2,1,0:T(8,128)(2,1)}), bf16[64,336,128]{2,1,0:T(8,128)(2,1)}, u32[]{:S(2)}, u32[]{:S(2)}) async-start(bf16[64,336,128]{2,1,0:T(8,128)(2,1)} %splat.1), calls=%async_computation.1 | async-start | bytes 11010048 | tf_op jit(solution)/shard_map/all_to_all | solution.py:320
  143.2 164.3 %all-gather.7.cloned.1.call-start = ((), (), s32[]{:S(2)}) async-start(), calls=%async_computation.10 | async-start | bytes 1474560 | tf_op jit(solution)/shard_map/all_gather | solution.py:312
  148.3 124.0 %copy-start.1 = (s32[2,64]{1,0:T(2,128)S(1)}, s32[2,64]{1,0:T(2,128)}, u32[]{:S(2)}) copy-start(s32[2,64]{1,0:T(2,128)} %param.13) | copy-start | bytes 1540
  267.6 20.9 %all-to-all-start.3 = ((bf16[4,192,760]{2,1,0:T(8,128)(2,1)}), bf16[4,192,760]{2,1,0:T(8,128)(2,1)S(1)}, u32[]{:S(2)}, u32[]{:S(2)}) async-start(bf16[4,192,760]{2,1,0:T(8,128)(2,1)} %copy.34), calls=%async_computation.3 | async-start | bytes 2359296 | tf_op jit(solution)/shard_map/all_to_all | solution.py:316
  288.5 17.5 %all-to-all-start.2 = ((bf16[4,760,192]{1,2,0:T(8,128)(2,1)}), bf16[4,760,192]{1,2,0:T(8,128)(2,1)S(1)}, u32[]{:S(2)}, u32[]{:S(2)}) async-start(bf16[4,760,192]{1,2,0:T(8,128)(2,1)} %copy.32), calls=%async_computation.2 | async-start | bytes 2359296 | tf_op jit(solution)/shard_map/all_to_all | solution.py:322
  346.4 11.5 %copy-start.2 = (bf16[760,768]{1,0:T(8,128)(2,1)S(1)}, bf16[760,768]{1,0:T(8,128)(2,1)}, u32[]{:S(2)}) copy-start(bf16[760,768]{1,0:T(8,128)(2,1)} %get-tuple-element.5) | copy-start | bytes 3502084
  346.4 254.0 %all-to-all-start.5 = ((bf16[64,336,128]{2,1,0:T(8,128)(2,1)}), bf16[64,336,128]{2,1,0:T(8,128)(2,1)}, u32[]{:S(2)}, u32[]{:S(2)}) async-start(bf16[64,336,128]{2,1,0:T(8,128)(2,1)} %pack_grads.1), calls=%async_computation.5 | async-start | bytes 11010048 | tf_op jit(solution)/shard_map/all_to_all | solution.py:326
  357.9 37.3 %reduce-scatter.2.cloned.1.call-start = ((), (), s32[]{:S(2)}) async-start(), calls=%async_computation.7 | async-start | bytes 2949120 | tf_op jit(solution)/shard_map/reduce_scatter | solution.py:330
  360.4 238.0 %all-reduce.4.cloned.1.call-start = ((), (), s32[]{:S(2)}) async-start(), calls=%async_computation.8 | async-start | bytes 1179648 | tf_op jit(solution)/shard_map/psum | solution.py:331
Sparse Core Ops, SparseCore 0:
  61.6 50.9 all-gather.4
  145.8 26.8 all-gather.6
  361.8 33.2 reduce-scatter.1
  398.4 199.9 all-reduce.3

commit v2 on v1

v2 whole, which is shorter than its diff:
```python
import functools

import jax
import jax.numpy as jnp
from jax import lax
from jax.experimental import pallas as pl
from jax.experimental.pallas import tpu as pltpu
from jax.sharding import PartitionSpec as P

GRID = 37
BAND = 2
BLOCK = 128
CAP = 3
ROWS = BAND * GRID
PIECE = 24
SLOT = 112
LINE = 40
STEP = 8
STRIDE = 27
LAG = 12
MESH = pl.DeviceIdType.MESH
SMEM = functools.partial(pl.BlockSpec, memory_space=pltpu.SMEM)
NT = (((1,), (1,)), ((), ()))
TN = (((0,), (0,)), ((), ()))
VMEM_LIMIT = 60 * 1024 * 1024


def params(**kw):
    return pltpu.CompilerParams(vmem_limit_bytes=VMEM_LIMIT, **kw)


def slot_plan(owners, peer_count, capacity):
    total_requests = owners.shape[0]
    positions = jnp.arange(total_requests, dtype=jnp.int32)
    earlier = (owners[:, None] == owners[None, :]) & (positions[None, :] < positions[:, None])
    slot_rank = jnp.sum(earlier.astype(jnp.int32), axis=1)
    target = owners * capacity + slot_rank
    slot_ids = jnp.arange(peer_count * capacity, dtype=jnp.int32)
    matches = target[None, :] == slot_ids[:, None]
    source = jnp.sum(jnp.where(matches, positions[None, :], 0), axis=1)
    filled = jnp.any(matches, axis=1)
    return source, filled.astype(jnp.int32)


def peer_at(me, i, peers):
    return (me + i * STRIDE) % peers


def greet(me, feat, peers):
    barrier = pltpu.get_barrier_semaphore()

    def hello(i, carry):
        pl.semaphore_signal(barrier, inc=1, device_id=(peer_at(me, i, peers), feat), device_id_type=MESH)
        return carry

    lax.fori_loop(1, peers, hello, 0)
    for k in range(1, 4):
        pl.semaphore_signal(barrier, inc=1, device_id=(me, (feat + k) % 4), device_id_type=MESH)
    pl.semaphore_wait(barrier, peers + 2)


def remote(src, dst, send, recv, view, feat):
    return pltpu.make_async_remote_copy(
        src_ref=src, dst_ref=dst, send_sem=send, recv_sem=recv, device_id=(view, feat), device_id_type=MESH
    )


def wait_bytes(ref, sem):
    pltpu.make_async_copy(ref, ref, sem).wait()


def pack_weights_kernel(source, filled, local, weights, out, tags):
    step = pl.program_id(0)
    lane = lax.broadcasted_iota(jnp.int32, (1, BLOCK), 1)

    def one(i, carry):
        tag = jnp.zeros((1, BLOCK), jnp.int32)
        for s in range(CAP):
            t = (step * STEP + i) * CAP + s
            src = source[t]
            piece = jnp.where(filled[t] > 0, weights[src].astype(jnp.float32), 0.0)
            out[i, pl.ds(s * PIECE, PIECE), :] = piece.astype(jnp.bfloat16)
            tag = jnp.where(lane == s, local[src], tag)
        tags[i] = tag
        return carry

    lax.fori_loop(0, STEP, one, 0)


def pack_weights(source, filled, local, weights, peers):
    return pl.pallas_call(
        pack_weights_kernel,
        out_shape=(
            jax.ShapeDtypeStruct((peers, CAP * PIECE, BLOCK), jnp.bfloat16),
            jax.ShapeDtypeStruct((peers, 1, BLOCK), jnp.int32),
        ),
        grid=(peers // STEP,),
        in_specs=[SMEM(), SMEM(), SMEM(), pl.BlockSpec(weights.shape, lambda i: (0, 0, 0))],
        out_specs=(
            pl.BlockSpec((STEP, CAP * PIECE, BLOCK), lambda i: (i, 0, 0)),
            pl.BlockSpec((STEP, 1, BLOCK), lambda i: (i, 0, 0)),
        ),
        compiler_params=params(),
        name="pack_weights",
    )(source, filled, local, weights)


def slot_weights(pieces, i, s):
    base = s * PIECE
    parts = [pieces[f, i, pl.ds(base, PIECE), :] for f in range(3)]
    parts.append(pieces[3, i, pl.ds(base, 8), :])
    return jnp.concatenate([p.astype(jnp.float32) for p in parts], axis=0).astype(jnp.bfloat16)


def forward_kernel(
    packed, tags, points, arrived, pieces_out, tags_out,
    pieces, tags_in, tags_s, send, buf,
    w_send, w_recv, t_send, t_recv, l_sem, r_send, r_recv, c_send, c_recv, own,
):
    me, feat = lax.axis_index("view"), lax.axis_index("feat")
    peers = packed.shape[0]
    lane = lax.broadcasted_iota(jnp.int32, (GRID, BLOCK), 1)

    own_piece = pltpu.make_async_copy(packed.at[me], pieces.at[feat, me], own.at[0])
    own_piece.start()
    own_tag = pltpu.make_async_copy(tags.at[me], tags_in.at[me], own.at[1])
    own_tag.start()
    greet(me, feat, peers)

    def weights_to(p, at):
        return remote(packed.at[p], pieces.at[feat, at], w_send, w_recv.at[at], p, feat)

    def tags_to(p, at):
        return remote(tags.at[p], tags_in.at[at], t_send, t_recv.at[at], p, feat)

    def relay(q, k):
        return remote(
            pieces.at[feat, q], pieces.at[feat, q], r_send.at[k - 1], r_recv.at[k - 1, q], me, (feat + k) % 4
        )

    def relayed(q, k):
        came = (feat + 4 - k) % 4
        return remote(pieces.at[came, q], pieces.at[came, q], r_send.at[k - 1], r_recv.at[k - 1, q], me, came)

    def tag_copy(q):
        return pltpu.make_async_copy(tags_in.at[q], tags_s.at[q], l_sem.at[q])

    def contrib_to(q):
        return remote(send.at[q], arrived.at[me], c_send, c_recv, q, feat)

    def first(i, carry):
        p = peer_at(me, i, peers)
        tags_to(p, me).start()
        weights_to(p, me).start()
        return carry

    lax.fori_loop(1, peers, first, 0)

    def pass_on(q):
        for k in (1, 3, 2):
            relay(q, k).start()
        tag_copy(q).start()

    def stage_a(i, carry):
        q = peer_at(me, peers - i, peers)
        tags_to(q, q).wait_recv()
        weights_to(q, q).wait_recv()
        pass_on(q)
        return carry

    def product(q):
        for k in (1, 2, 3):
            relayed(q, k).wait_recv()
        tag_copy(q).wait()
        for s in range(CAP):
            block = points[tags_s[q, 0, s]]
            wide = jnp.concatenate([block, block[128:192]], axis=0)
            result = lax.dot_general(slot_weights(pieces, q, s), wide, NT, preferred_element_type=jnp.float32)
            rest = result[:, 128:256]
            buf[s, 0:80, :] = result[:, 0:128]
            buf[s, ROWS : ROWS + GRID, :] = jnp.where(lane < 64, rest[0:GRID], rest[GRID:ROWS])
            buf[s, SLOT - 1 : SLOT, :] = jnp.zeros((1, BLOCK), jnp.float32)
            send[q, pl.ds(s * SLOT, SLOT), :] = buf[s].astype(jnp.bfloat16)

    def stage_b(i, carry):
        product(peer_at(me, peers - i, peers))

        @pl.when(i > 1)
        def _():
            contrib_to(peer_at(me, peers - i + 1, peers)).start()

        return carry

    own_piece.wait()
    own_tag.wait()
    pass_on(me)
    lax.fori_loop(1, LAG, stage_a, 0)

    def both(i, carry):
        stage_a(i, carry)
        return stage_b(i - LAG + 1, carry)

    lax.fori_loop(LAG, peers, both, 0)
    lax.fori_loop(peers - LAG + 1, peers, stage_b, 0)
    product(me)
    contrib_to(peer_at(me, 1, peers)).start()
    keep = pltpu.make_async_copy(pieces, pieces_out, own.at[0])
    keep.start()
    keep_tags = pltpu.make_async_copy(tags_in, tags_out, own.at[1])
    keep_tags.start()
    own_contrib = pltpu.make_async_copy(send.at[me], arrived.at[me], own.at[2])
    own_contrib.start()

    others = pl.ds(0, peers - 1)
    wait_bytes(packed.at[others], w_send)
    wait_bytes(tags.at[others], t_send)
    for k in range(3):
        wait_bytes(packed, r_send.at[k])
    wait_bytes(send.at[others], c_send)
    wait_bytes(send.at[others], c_recv)
    keep.wait()
    keep_tags.wait()
    own_contrib.wait()


def forward_exchange(packed, tags, points):
    peers = packed.shape[0]
    whole = pl.BlockSpec(memory_space=pltpu.VMEM)
    dma = pltpu.SemaphoreType.DMA
    slots = (peers, CAP * SLOT, BLOCK)
    return pl.pallas_call(
        forward_kernel,
        out_shape=(
            jax.ShapeDtypeStruct(slots, jnp.bfloat16),
            jax.ShapeDtypeStruct((4,) + packed.shape, jnp.bfloat16),
            jax.ShapeDtypeStruct(tags.shape, jnp.int32),
        ),
        in_specs=[whole, whole, whole],
        out_specs=(pl.BlockSpec(memory_space=pl.ANY),) * 3,
        scratch_shapes=[
            pltpu.VMEM((4,) + packed.shape, jnp.bfloat16),
            pltpu.VMEM(tags.shape, jnp.int32),
            pltpu.SMEM(tags.shape, jnp.int32),
            pltpu.VMEM(slots, jnp.bfloat16),
            pltpu.VMEM((CAP, SLOT, BLOCK), jnp.float32),
            dma, dma((peers,)), dma, dma((peers,)), dma((peers,)),
            dma((3,)), dma((3, peers)), dma, dma, dma((3,)),
        ],
        compiler_params=params(collective_id=0, has_side_effects=True),
        name="forward_exchange",
    )(packed, tags, points)


def render_kernel(lines, source, line_of, arrived, out, acc):
    step = pl.program_id(0)
    lane = lax.broadcasted_iota(jnp.int32, (GRID, BLOCK), 1)

    @pl.when(step == 0)
    def _():
        acc[...] = jnp.zeros_like(acc)

    def one(i, carry):
        for s in range(CAP):
            at = line_of[source[(step * STEP + i) * CAP + s]] + 1
            acc[at] += arrived[i, pl.ds(s * SLOT, SLOT), :].astype(jnp.float32)
        return carry

    lax.fori_loop(0, STEP, one, 0)

    @pl.when(step == pl.num_programs(0) - 1)
    def _():
        out[...] = jnp.zeros_like(out)
        pairs = pl.ds(ROWS, GRID)

        def finish(k, carry):
            f, m = k // 10, k % 10
            for half in range(2):
                at = f * 20 + half * 10 + m
                out[f, half, m, 0:GRID, :] = (acc[at + 1, 0:GRID, :] + acc[at, GRID:ROWS, :]).astype(jnp.bfloat16)
            low, high = f * 20 + m, f * 20 + 10 + m
            turned = pltpu.roll(jnp.where(lane < 64, acc[high + 1, pairs, :], acc[low, pairs, :]), 64, 1)
            straight = jnp.where(lane < 64, acc[low + 1, pairs, :], acc[high, pairs, :])
            out[f, 2, m, 0:GRID, :] = (turned + straight).astype(jnp.bfloat16)
            return carry

        lax.fori_loop(0, 40, finish, 0)


def render(source, line_of, arrived):
    peers = arrived.shape[0]
    shape = (4, 3, 10, LINE, BLOCK)
    return pl.pallas_call(
        functools.partial(render_kernel, 80),
        out_shape=jax.ShapeDtypeStruct(shape, jnp.bfloat16),
        grid=(peers // STEP,),
        in_specs=[SMEM(), SMEM(), pl.BlockSpec((STEP, CAP * SLOT, BLOCK), lambda i: (i, 0, 0))],
        out_specs=pl.BlockSpec(shape, lambda i: (0, 0, 0, 0, 0)),
        scratch_shapes=[pltpu.VMEM((81, SLOT, BLOCK), jnp.float32)],
        compiler_params=params(),
        name="render",
    )(source, line_of, arrived)


def widened(image, f, lines):
    count = lines * LINE
    lane = lax.broadcasted_iota(jnp.int32, (count, BLOCK), 1)
    pairs = image[f, 2].reshape(count, BLOCK)
    zero = jnp.zeros_like(pairs)
    upper = jnp.concatenate([image[f, 0].reshape(count, BLOCK), jnp.where(lane < 64, pairs, zero)], axis=1)
    lower = jnp.concatenate([image[f, 1].reshape(count, BLOCK), jnp.where(lane < 64, zero, pairs)], axis=1)
    return jnp.concatenate([upper, lower], axis=0)


def compare_kernel(rendered, head, target, grad_image, grad_proj):
    count, width = 2 * LINE, target.shape[-1]
    lane = lax.broadcasted_iota(jnp.int32, (count, BLOCK), 1)
    projected = jnp.zeros((2 * count, width), jnp.float32)
    for f in range(4):
        projected += jnp.dot(widened(rendered, f, 2), head[f], preferred_element_type=jnp.float32)
    scale = jnp.sqrt(jnp.sum(projected * projected, axis=1, keepdims=True) / width + 1e-06)
    inverse = 1.0 / scale
    normed = projected * inverse
    residual = normed - target[...].reshape(2 * count, width).astype(jnp.float32)
    row_dot = jnp.sum(residual * normed, axis=1, keepdims=True) / width
    grad = ((residual - normed * row_dot) * inverse).astype(jnp.bfloat16)
    grad_proj[...] = grad.reshape(grad_proj.shape)
    for f in range(4):
        image = lax.dot_general(grad, head[f], NT, preferred_element_type=jnp.float32)
        for half in range(2):
            grad_image[f, half] = image[half * count : (half + 1) * count, 0:128].astype(jnp.bfloat16).reshape(2, LINE, BLOCK)
        pairs = jnp.where(lane < 64, image[0:count, 128:256], image[count : 2 * count, 128:256])
        grad_image[f, 2] = pairs.astype(jnp.bfloat16).reshape(2, LINE, BLOCK)


def compare(rendered, head, target):
    width = target.shape[-1]
    image = pl.BlockSpec((4, 3, 2, LINE, BLOCK), lambda i: (0, 0, i, 0, 0))
    wide = pl.BlockSpec((2, 2, LINE, width), lambda i: (0, i, 0, 0))
    return pl.pallas_call(
        compare_kernel,
        out_shape=(
            jax.ShapeDtypeStruct(rendered.shape, jnp.bfloat16),
            jax.ShapeDtypeStruct(target.shape, jnp.bfloat16),
        ),
        grid=(5,),
        in_specs=[image, pl.BlockSpec(head.shape, lambda i: (0, 0, 0)), wide],
        out_specs=(image, wide),
        compiler_params=params(),
        name="compare",
    )(rendered, head, target)


def head_kernel(rendered, grad_proj, out):
    rows = widened(rendered, 0, 10)
    for j in range(6):
        grad = grad_proj[:, :, :, j * BLOCK : (j + 1) * BLOCK].reshape(rows.shape[0], BLOCK)
        part = lax.dot_general(rows, grad, TN, preferred_element_type=jnp.float32)
        out[0, j * 6 : j * 6 + 4] = part[0:128].reshape(4, 32, BLOCK)
        out[0, j * 6 + 4 : j * 6 + 6] = (part[128:192] + part[192:256]).reshape(2, 32, BLOCK)


def head_products(rendered, grad_proj):
    rows = 4 * 10 * LINE * 256
    return pl.pallas_call(
        head_kernel,
        out_shape=jax.ShapeDtypeStruct((4, 36, 32, BLOCK), jnp.float32),
        grid=(4,),
        in_specs=[
            pl.BlockSpec((1,) + rendered.shape[1:], lambda i: (i, 0, 0, 0, 0)),
            pl.BlockSpec(grad_proj.shape, lambda i: (0, 0, 0, 0)),
        ],
        out_specs=pl.BlockSpec((1, 36, 32, BLOCK), lambda i: (i, 0, 0, 0)),
        compiler_params=params(),
        name="head_products",
    )(rendered, grad_proj)


def line_slots_kernel(image, slots, buf):
    lane = lax.broadcasted_iota(jnp.int32, (GRID, BLOCK), 1)

    def tail(at):
        return image[at // 20, 2, at % 10, :, :].astype(jnp.float32)[0:GRID]

    def build(k, carry):
        low = k + 1
        low_half = (low // 10) % 2
        own_half = (k // 10) % 2
        own_main = image[k // 20, own_half, k % 10, :, :].astype(jnp.float32)
        low_main = image[low // 20, low_half, low % 10, :, :].astype(jnp.float32)
        buf[0:GRID, :] = own_main[0:GRID]
        buf[GRID:ROWS, :] = low_main[0:GRID]
        own, lower = tail(k), tail(low)
        own = jnp.where(own_half == 0, own, pltpu.roll(own, 64, 1))
        lower = jnp.where(low_half == 1, lower, pltpu.roll(lower, 64, 1))
        buf[ROWS : ROWS + GRID, :] = jnp.where(lane < 64, own, lower)
        slots[k] = buf[...].astype(jnp.bfloat16)
        return carry

    buf[...] = jnp.zeros_like(buf)
    lax.fori_loop(0, slots.shape[0], build, 0)


def line_slots(image, lines):
    whole = pl.BlockSpec(memory_space=pltpu.VMEM)
    return pl.pallas_call(
        line_slots_kernel,
        out_shape=jax.ShapeDtypeStruct((lines, SLOT, BLOCK), jnp.bfloat16),
        in_specs=[whole],
        out_specs=whole,
        scratch_shapes=[pltpu.VMEM((SLOT, BLOCK), jnp.float32)],
        compiler_params=params(),
        name="line_slots",
    )(image)


def backward_kernel(
    source, line_of, slots, head_part, landed, head_out,
    send, head_in, share, share_in, total, total_in,
    g_send, g_recv, x_send, x_recv, a_send, a_recv, b_send, b_recv, own,
):
    me, feat = lax.axis_index("view"), lax.axis_index("feat")
    peers = send.shape[0]
    owners = share.shape[0]
    greet(me, feat, peers)

    def grads_to(p):
        return remote(send.at[p], landed.at[me], g_send, g_recv, p, feat)

    def across(k):
        return remote(head_part.at[(feat + k) % 4], head_in.at[k - 1], x_send.at[k - 1], x_recv.at[k - 1], me, (feat + k) % 4)

    def pack(p):
        for s in range(CAP):
            send[p, pl.ds(s * SLOT, SLOT), :] = slots[line_of[source[p * CAP + s]]]

    def packed_to(i, carry):
        pack(peer_at(me, i, peers))

        @pl.when(i > 1)
        def _():
            grads_to(peer_at(me, i - 1, peers)).start()

        return carry

    for k in (1, 3, 2):
        across(k).start()
    middle = peers // 2
    lax.fori_loop(1, middle, packed_to, 0)

    for k in (1, 2, 3):
        across(k).wait_recv()

    def add(t, carry):
        value = head_part[feat, t] + head_in[0, t] + head_in[1, t] + head_in[2, t]
        share[t] = value.astype(jnp.bfloat16)
        return carry

    lax.fori_loop(0, owners, add, 0)
    lax.fori_loop(middle, middle + 4, packed_to, 0)

    def share_to(p):
        return remote(share.at[p], share_in.at[me], a_send.at[p], a_recv, p, feat)

    def give(i, carry):
        p = peer_at(me, i, peers)

        @pl.when(p < owners)
        def _():
            share_to(p).start()

        return carry

    lax.fori_loop(1, peers, give, 0)
    lax.fori_loop(middle + 4, peers, packed_to, 0)
    pack(me)
    grads_to(peer_at(me, peers - 1, peers)).start()
    own_grads = pltpu.make_async_copy(send.at[me], landed.at[me], own.at[0])
    own_grads.start()
    others = pl.ds(0, peers - 1)

    def total_to(p, at):
        return remote(total, total_in.at[at], b_send, b_recv.at[at], p, feat)

    @pl.when(me < owners)
    def _():
        mine = pltpu.make_async_copy(share.at[me], share_in.at[me], own.at[1])
        mine.start()
        mine.wait()
        wait_bytes(share_in.at[others], a_recv)

        def gather(q, value):
            return value + share_in[q].astype(jnp.float32)

        value = lax.fori_loop(0, peers, gather, jnp.zeros(total.shape, jnp.float32))
        total[...] = value.astype(jnp.bfloat16)
        kept = pltpu.make_async_copy(total, total_in.at[me], own.at[1])
        kept.start()
        kept.wait()

        def tell(i, carry):
            total_to(peer_at(me, i, peers), me).start()
            return carry

        lax.fori_loop(1, peers, tell, 0)
        wait_bytes(share_in.at[others], b_send)

    def sent(i, carry):
        p = peer_at(me, i, peers)

        @pl.when(p < owners)
        def _():
            share_to(p).wait_send()
            total_to(p, p).wait_recv()

        return carry

    lax.fori_loop(1, peers, sent, 0)
    result = pltpu.make_async_copy(total_in, head_out, own.at[1])
    result.start()
    for k in (1, 2, 3):
        across(k).wait_send()
    wait_bytes(send.at[others], g_send)
    wait_bytes(send.at[others], g_recv)
    own_grads.wait()
    result.wait()


def backward_exchange(source, line_of, slots, head_part, peers):
    whole = pl.BlockSpec(memory_space=pltpu.VMEM)
    dma = pltpu.SemaphoreType.DMA
    owners = head_part.shape[1]
    tile = head_part.shape[2:]
    shape = (peers, CAP * SLOT, BLOCK)
    return pl.pallas_call(
        backward_kernel,
        out_shape=(
            jax.ShapeDtypeStruct(shape, jnp.bfloat16),
            jax.ShapeDtypeStruct((owners,) + tile, jnp.bfloat16),
        ),
        in_specs=[SMEM(), SMEM(), whole, whole],
        out_specs=(pl.BlockSpec(memory_space=pl.ANY),) * 2,
        scratch_shapes=[
            pltpu.VMEM(shape, jnp.bfloat16),
            pltpu.VMEM((3, owners) + tile, jnp.float32),
            pltpu.VMEM((owners,) + tile, jnp.bfloat16),
            pltpu.VMEM((peers,) + tile, jnp.bfloat16),
            pltpu.VMEM(tile, jnp.bfloat16),
            pltpu.VMEM((owners,) + tile, jnp.bfloat16),
            dma, dma, dma((3,)), dma((3,)), dma((owners,)), dma, dma, dma((owners,)), dma((2,)),
        ],
        compiler_params=params(collective_id=1, has_side_effects=True),
        name="backward_exchange",
    )(source, line_of, slots, head_part)


def unsplat_kernel(ids, pieces, arrived, out, acc):
    step = pl.program_id(0)
    lane = lax.broadcasted_iota(jnp.int32, (GRID, BLOCK), 1)

    @pl.when(step == 0)
    def _():
        acc[...] = jnp.zeros_like(acc)

    def one(i, carry):
        for s in range(CAP):
            at = ids[(step * STEP + i) * CAP + s]
            weights = slot_weights(pieces, i, s)
            slot = arrived[i, pl.ds(s * SLOT, SLOT), :].astype(jnp.float32)
            pair = slot[ROWS : ROWS + GRID]
            rest = jnp.concatenate(
                [jnp.where(lane < 64, pair, 0.0), jnp.where(lane < 64, 0.0, pair), jnp.zeros((6, BLOCK), jnp.float32)], axis=0
            )
            both = jnp.concatenate([slot[0:80], rest], axis=1).astype(jnp.bfloat16)
            product = lax.dot_general(both, weights, TN, preferred_element_type=jnp.float32)
            acc[at, 0:128, :] += product[0:128].astype(jnp.bfloat16).astype(jnp.float32)
            acc[at, 128:192, :] += (product[128:192] + product[192:256]).astype(jnp.bfloat16).astype(jnp.float32)
        return carry

    lax.fori_loop(0, STEP, one, 0)

    @pl.when(step == pl.num_programs(0) - 1)
    def _():
        out[...] = acc[...].astype(jnp.bfloat16)


def unsplat(ids, pieces, arrived, shape):
    peers = arrived.shape[0]
    return pl.pallas_call(
        unsplat_kernel,
        out_shape=jax.ShapeDtypeStruct(shape, jnp.bfloat16),
        grid=(peers // STEP,),
        in_specs=[
            SMEM(),
            pl.BlockSpec((4, STEP, CAP * PIECE, BLOCK), lambda i: (0, i, 0, 0)),
            pl.BlockSpec((STEP, CAP * SLOT, BLOCK), lambda i: (i, 0, 0)),
        ],
        out_specs=pl.BlockSpec(shape, lambda i: (0, 0, 0)),
        scratch_shapes=[pltpu.VMEM(shape, jnp.float32)],
        compiler_params=params(),
        name="unsplat",
    )(ids, pieces, arrived)


def per_device(points, head_weight, teacher, splat_weight, block_owner, block_local, block_row):
    peers = lax.axis_size("view")
    feat = lax.axis_index("feat")
    local_width = points.shape[1]
    views, visible = splat_weight.shape[:2]
    requests = views * visible
    lines = views * GRID
    rows = 20 * LINE

    source, filled = slot_plan(block_owner.reshape(requests), peers, CAP)
    local = block_local.reshape(requests)
    line_of = (block_row + jnp.arange(views, dtype=jnp.int32)[:, None] * GRID).reshape(requests)

    mine = lax.dynamic_slice_in_dim(
        jnp.pad(splat_weight, ((0, 0), (0, 0), (0, 4 * PIECE - ROWS), (0, 0))), feat * PIECE, PIECE, axis=2
    ).reshape(requests, PIECE, BLOCK)
    packed, tags = pack_weights(source, filled, local, mine, peers)

    head = lax.all_gather(head_weight, "feat", axis=0)
    head = jnp.concatenate([head, head[:, 128:192]], axis=1)
    wanted = jnp.pad(
        teacher.reshape(local_width, lines, GRID), ((0, 0), (0, 80 - lines), (0, LINE - GRID))
    ).reshape(local_width, 4, rows)
    target = lax.all_to_all(wanted.transpose(1, 0, 2), "feat", split_axis=0, concat_axis=0, tiled=True)
    target = target.reshape(4 * local_width, rows).T.reshape(2, 10, LINE, 4 * local_width)

    arrived, pieces, tags_in = forward_exchange(packed, tags, points)
    ids = tags_in[:, 0, :CAP].reshape(peers * CAP)
    image = render(source, line_of, arrived)
    rendered = lax.all_to_all(image, "feat", split_axis=0, concat_axis=0, tiled=True)
    grad_image, grad_proj = compare(rendered, head, target)
    grad_rows = lax.all_to_all(grad_image, "feat", split_axis=0, concat_axis=0, tiled=True)
    head_part = head_products(rendered, grad_proj)
    slots = line_slots(grad_rows, lines)
    landed, head_sum = backward_exchange(source, line_of, slots, head_part, peers)
    grad_points = unsplat(ids, pieces, landed, points.shape)
    head_grad = head_sum.reshape(6, local_width, BLOCK).transpose(1, 0, 2).reshape(local_width, 6 * BLOCK)
    return grad_points, head_grad.astype(jnp.float32) / (views * peers * GRID)


def solution(mesh):
    placed = (
        P("view", "feat", None),
        P("feat", None),
        P("feat", "view", None),
        P("view", None, None, None),
        P("view", None, None),
        P("view", None),
        P("view", None),
    )
    return jax.shard_map(
        per_device,
        mesh=mesh,
        in_specs=placed,
        out_specs=(P("view", "feat", None), P("feat", None)),
        check_vma=False,
    )
```

time: 628 us -> 447 us (0.71)
  waiting for transfers between devices: 420 us -> 18.4 us
  Pallas kernels: 75.4 us -> 373 us
  blocking collectives: 59.3 us -> 0 us
  starting transfers between devices: 31.8 us -> 15.8 us
    pallas_call x4 -> x6, Pallas kernels: 46.6 us -> 343 us  [the longest x1 162 us: forward_exchange(): pl.pallas_call(forward_kernel, out_shape=(jax.ShapeDtypeStruct(slots, jnp...]
    psum x1 -> x0, waiting for transfers between devices: 203 us -> none  [per_device(): head_grad = lax.psum(head_part, 'view') / (views * peers * GRID)]
    all_to_all x2 -> x1, waiting for transfers between devices: 119 us -> 7.48 us  [per_device(): lax.all_to_all(grad_image, 'feat', split_axis=0, concat_axis=0, tiled=True)]
    all_to_all x2 -> x0, blocking collectives: 59.3 us -> none  [the longest x1 43.9 us: per_device(): lax.all_to_all(packed, 'view', split_axis=0, concat_axis=0, tiled=True)]
    all_gather x1 -> x0, waiting for transfers between devices: 51.1 us -> none  [per_device(): pieces = lax.all_gather(swapped, 'feat', axis=0)]
    reduce_scatter x1 -> x0, waiting for transfers between devices: 34.6 us -> none  [per_device(): lax.psum_scatter(head_part, 'feat', scatter_dimension=0, tiled=False)]
    all_to_all x2 -> x1, starting transfers between devices: 22.3 us -> 5.08 us  [per_device(): lax.all_to_all(grad_image, 'feat', split_axis=0, concat_axis=0, tiled=True)]
  transfers between devices with their start and end apart: 8 -> 4, of which waited for: 5 -> 2; matrix products, arithmetic and copies ran while one was open for 2% -> 4% of each run, Pallas kernels for 2% -> 41%
where the time goes in v2:
time: 447 us; the launch traced here: 443 us
  Pallas kernels  373 us (83%)
  waiting for transfers between devices  18.4 us (4%)
  local copies, waits for them, and re-layouts  16.2 us (4%)
  starting transfers between devices  15.8 us (4%)
  between operations  14.1 us (3%)
  other arithmetic  5.15 us (1%)
    pallas_call x1, Pallas kernels, forward_exchange(): pl.pallas_call(forward_kernel, out_shape=(jax.ShapeDtypeStruct(slots, jnp...  162 us
    pallas_call x1, Pallas kernels, backward_exchange(): pl.pallas_call(backward_kernel, out_shape=(jax.ShapeDtypeStruct(shape, jn...  151 us
    pallas_call x1, Pallas kernels, unsplat(): pl.pallas_call(unsplat_kernel, out_shape=jax.ShapeDtypeStruct(shape, jnp....  20.3 us
    pallas_call x1, Pallas kernels, render(): pl.pallas_call(functools.partial(render_kernel, 80), out_shape=jax.ShapeD...  10.4 us
    all_to_all x1, waiting for transfers between devices, per_device(): lax.all_to_all(image, 'feat', split_axis=0, concat_axis=0, tiled=True)  10.3 us
    pallas_call x1, Pallas kernels, line_slots(): pl.pallas_call(line_slots_kernel, out_shape=jax.ShapeDtypeStruct((lines,...  9.48 us
    pallas_call x1, Pallas kernels, compare(): pl.pallas_call(compare_kernel, out_shape=(jax.ShapeDtypeStruct(rendered.s...  9.46 us
  transfers between devices with their start and end apart: 4, of which 2 were waited for; matrix products, arithmetic and copies ran while one was open for 4% of the time, Pallas kernels for 41%

profile of v2, /device:TPU:2, one launch (start us, length us, event | category | flops | bytes accessed | tf_op | source)
XLA Modules:
  0.0 442.8 jit_solution(1722160866093863363)
XLA Ops:
  7.2 0.0 all-gather.3.cloned.1.call-start
  7.2 0.7 all-gather.3.cloned.1.call-update
  7.9 2.9 copy.27
  10.8 0.7 reshape.55
  11.5 0.3 pad.9
  11.8 1.6 copy.28
  13.4 0.0 copy-start.5
  13.4 0.0 copy-start.4
  13.4 0.0 copy-start.3
  13.4 5.9 %all-to-all-start.1 = ((bf16[4,192,800]{2,1,0:T(8,128)(2,1)}), bf16[4,192,800]{2,1,0:T(8,128)(2,1)S(1)}, u32[]{:S(2)}, u32[]{:S(2)}) async-start(bf16[4,192,800]{2,1,0:T(8,128)(2,1)} %copy.28), calls=%async_computation.1 | async-start | bytes 2752512 | tf_op jit(solution)/shard_map/all_to_all | solution.py:627
  19.3 0.0 copy-done.5
  19.3 0.6 reshape.52.local
  19.9 0.0 copy-done.4
  19.9 0.1 broadcast_add_fusion
  20.0 0.6 reshape.54.line_of
  20.6 0.0 copy-done.3
  20.6 0.1 copy.25
  20.7 0.1 reshape.51
  20.8 0.2 convert_reduce_fusion
  21.0 0.1 fusion
  21.1 0.5 convert_element_type.17.filled
  21.6 1.3 pad_dynamic-slice_fusion
  23.0 1.4 copy.26
  24.4 0.7 select_reduce_fusion.source
  25.1 4.5 %pack_weights.1 = (bf16[64,72,128]{2,1,0:T(8,128)(2,1)}, s32[64,1,128]{2,1,0:T(1,128)}) custom-call(s32[192]{0:T(256)} %select_reduce_fusion.source, s32[192]{0:T(256)} %convert_element_type.17.filled, s32[128]{0:T(128)} %reshape.52.local, bf16[128,24,128]{2,1,0:T(8,128)(2,1)} %bitcast.20), custom_call_target="tpu_custom_call" | custom-call | tf_op jit(solution)/shard_map/pack_weights/pallas_call | solution.py:91
  29.6 161.5 %forward_exchange.1 = (bf16[64,336,128]{2,1,0:T(8,128)(2,1)}, bf16[4,64,72,128]{3,2,1,0:T(8,128)(2,1)}, s32[64,1,128]{2,1,0:T(1,128)}) custom-call(bf16[64,72,128]{2,1,0:T(8,128)(2,1)} %get-tuple-element.11.packed, s32[64,1,128]{2,1,0:T(1,128)} %get-tuple-element.12.tags, bf16[64,192,128]{2,1,0:T(8,128)(2,1)} %points.1), custom_call_target="tpu_custom_call" | custom-call | tf_op jit(solution)/shard_map/forward_exchange/pallas_call | solution.py:231
  191.1 10.4 %render.1 = bf16[4,3,10,40,128]{4,3,2,1,0:T(8,128)(2,1)} custom-call(s32[192]{0:T(256)} %select_reduce_fusion.source, s32[128]{0:T(128)} %reshape.54.line_of, bf16[64,336,128]{2,1,0:T(8,128)(2,1)} %get-tuple-element.15.arrived), custom_call_target="tpu_custom_call" | custom-call | tf_op jit(solution)/shard_map/render/pallas_call | solution.py:292
  201.5 0.0 all-to-all-done.1
  201.5 4.8 %all-to-all-start = ((bf16[4,3,10,40,128]{4,3,2,1,0:T(8,128)(2,1)}), bf16[4,3,10,40,128]{4,3,2,1,0:T(8,128)(2,1)S(1)}, u32[]{:S(2)}, u32[]{:S(2)}) async-start(bf16[4,3,10,40,128]{4,3,2,1,0:T(8,128)(2,1)} %render.1), calls=%async_computation | async-start | bytes 2457600 | tf_op jit(solution)/shard_map/all_to_all | solution.py:633
  206.3 1.5 copy.29
  207.7 1.0 slice.8
  208.8 2.5 pad_maximum_fusion.head
  211.3 10.3 %all-to-all-done.rendered = bf16[4,3,10,40,128]{4,3,2,1,0:T(8,128)(2,1)S(1)} async-done(((bf16[4,3,10,40,128]{4,3,2,1,0:T(8,128)(2,1)}), bf16[4,3,10,40,128]{4,3,2,1,0:T(8,128)(2,1)S(1)}, u32[]{:S(2)}, u32[]{:S(2)}) %all-to-all-start) | async-done | bytes 1228832 | tf_op jit(solution)/shard_map/all_to_all | solution.py:633
  221.6 1.0 copy-done
  222.6 9.5 %compare.3 = (bf16[4,3,10,40,128]{4,3,2,1,0:T(8,128)(2,1)}, bf16[2,10,40,768]{3,2,1,0:T(8,128)(2,1)}) custom-call(bf16[4,3,10,40,128]{4,3,2,1,0:T(8,128)(2,1)} %copy-done, bf16[4,256,768]{2,1,0:T(8,128)(2,1)} %pad_maximum_fusion.head, bf16[2,10,40,768]{3,2,1,0:T(8,128)(2,1)} %bitcast.19), custom_call_target="tpu_custom_call" | custom-call | tf_op jit(solution)/shard_map/compare/pallas_call | solution.py:339
  232.1 5.1 %all-to-all-start.2 = ((bf16[4,3,10,40,128]{4,3,2,1,0:T(8,128)(2,1)}), bf16[4,3,10,40,128]{4,3,2,1,0:T(8,128)(2,1)S(1)}, u32[]{:S(2)}, u32[]{:S(2)}) async-start(bf16[4,3,10,40,128]{4,3,2,1,0:T(8,128)(2,1)} %get-tuple-element.16), calls=%async_computation.2 | async-start | bytes 2457600 | tf_op jit(solution)/shard_map/all_to_all | solution.py:635
  237.1 0.0 copy-done.2
  237.1 0.1 slice_reduce_fusion
  237.2 0.7 reshape_squeeze.3.ids
  237.9 6.2 %head_products.1.head_part = f32[4,36,32,128]{3,2,1,0:T(8,128)} custom-call(bf16[4,3,10,40,128]{4,3,2,1,0:T(8,128)(2,1)} %copy-done, bf16[2,10,40,768]{3,2,1,0:T(8,128)(2,1)} %get-tuple-element.17.grad_proj), custom_call_target="tpu_custom_call" | custom-call | tf_op jit(solution)/shard_map/head_products/pallas_call | solution.py:364
  244.1 7.5 %all-to-all-done.2.image = bf16[4,3,10,40,128]{4,3,2,1,0:T(8,128)(2,1)S(1)} async-done(((bf16[4,3,10,40,128]{4,3,2,1,0:T(8,128)(2,1)}), bf16[4,3,10,40,128]{4,3,2,1,0:T(8,128)(2,1)S(1)}, u32[]{:S(2)}, u32[]{:S(2)}) %all-to-all-start.2) | async-done | bytes 1228832 | tf_op jit(solution)/shard_map/all_to_all | solution.py:635
  251.6 1.0 copy-done.1
  252.6 9.5 %line_slots.1.slots = bf16[74,112,128]{2,1,0:T(8,128)(2,1)} custom-call(bf16[4,3,10,40,128]{4,3,2,1,0:T(8,128)(2,1)} %copy-done.1), custom_call_target="tpu_custom_call" | custom-call | tf_op jit(solution)/shard_map/line_slots/pallas_call | solution.py:405
  262.1 151.2 %backward_exchange.1 = (bf16[64,336,128]{2,1,0:T(8,128)(2,1)}, bf16[36,32,128]{2,1,0:T(8,128)(2,1)}) custom-call(s32[192]{0:T(256)} %select_reduce_fusion.source, s32[128]{0:T(128)} %reshape.54.line_of, bf16[74,112,128]{2,1,0:T(8,128)(2,1)} %line_slots.1.slots, f32[4,36,32,128]{3,2,1,0:T(8,128)} %head_products.1.head_part), custom_call_target="tpu_custom_call" | custom-call | tf_op jit(solution)/shard_map/backward_exchange/pallas_call | solution.py:534
  413.3 1.0 convert_multiply_fusion
  414.4 0.4 copy.30
  414.7 0.9 copy.33
  415.7 20.3 %unsplat.1 = bf16[64,192,128]{2,1,0:T(8,128)(2,1)} custom-call(s32[192]{0:T(256)} %reshape_squeeze.3.ids, bf16[4,64,72,128]{3,2,1,0:T(8,128)(2,1)} %get-tuple-element.14.pieces, bf16[64,336,128]{2,1,0:T(8,128)(2,1)} %get-tuple-element.18.arrived), custom_call_target="tpu_custom_call" | custom-call | tf_op jit(solution)/shard_map/unsplat/pallas_call | solution.py:588
  (6 shorter events, 0.0 us)
Async XLA Ops:
  7.2 200.6 %all-gather.3.cloned.1.call-start = ((), (), s32[]{:S(2)}) async-start(), calls=%async_computation.3 | async-start | bytes 1474560 | tf_op jit(solution)/shard_map/all_gather | solution.py:622
  13.4 5.9 %copy-start.5 = (s32[2,64]{1,0:T(2,128)S(1)}, s32[2,64]{1,0:T(2,128)}, u32[]{:S(2)}) copy-start(s32[2,64]{1,0:T(2,128)} %param.12) | copy-start | bytes 1540
  13.4 6.5 %copy-start.4 = (s32[2,64]{1,0:T(2,128)S(1)}, s32[2,64]{1,0:T(2,128)}, u32[]{:S(2)}) copy-start(s32[2,64]{1,0:T(2,128)} %param.13) | copy-start | bytes 1540
  13.4 7.2 %copy-start.3 = (s32[2,16,4]{1,2,0:T(4,128)S(1)}, s32[2,16,4]{1,2,0:T(4,128)}, u32[]{:S(2)}) copy-start(s32[2,16,4]{1,2,0:T(4,128)} %param.11) | copy-start | bytes 1540
  13.4 188.1 %all-to-all-start.1 = ((bf16[4,192,800]{2,1,0:T(8,128)(2,1)}), bf16[4,192,800]{2,1,0:T(8,128)(2,1)S(1)}, u32[]{:S(2)}, u32[]{:S(2)}) async-start(bf16[4,192,800]{2,1,0:T(8,128)(2,1)} %copy.28), calls=%async_computation.1 | async-start | bytes 2752512 | tf_op jit(solution)/shard_map/all_to_all | solution.py:627
  201.5 20.1 %all-to-all-start = ((bf16[4,3,10,40,128]{4,3,2,1,0:T(8,128)(2,1)}), bf16[4,3,10,40,128]{4,3,2,1,0:T(8,128)(2,1)S(1)}, u32[]{:S(2)}, u32[]{:S(2)}) async-start(bf16[4,3,10,40,128]{4,3,2,1,0:T(8,128)(2,1)} %render.1), calls=%async_computation | async-start | bytes 2457600 | tf_op jit(solution)/shard_map/all_to_all | solution.py:633
  221.6 1.0 copy-start
  232.1 5.1 %copy-start.2 = (s32[64,1,128]{2,1,0:T(1,128)S(1)}, s32[64,1,128]{2,1,0:T(1,128)}, u32[]{:S(2)}) copy-start(s32[64,1,128]{2,1,0:T(1,128)} %get-tuple-element.13) | copy-start | bytes 98308
  232.1 19.5 %all-to-all-start.2 = ((bf16[4,3,10,40,128]{4,3,2,1,0:T(8,128)(2,1)}), bf16[4,3,10,40,128]{4,3,2,1,0:T(8,128)(2,1)S(1)}, u32[]{:S(2)}, u32[]{:S(2)}) async-start(bf16[4,3,10,40,128]{4,3,2,1,0:T(8,128)(2,1)} %get-tuple-element.16), calls=%async_computation.2 | async-start | bytes 2457600 | tf_op jit(solution)/shard_map/all_to_all | solution.py:635
  251.6 1.0 copy-start.1
Sparse Core Ops, SparseCore 0:
  9.8 34.5 all-gather.2

commit v3 on v2

--- a/solution.py
+++ b/solution.py
@@ -113,9 +113,9 @@
 
 
 def forward_kernel(
-    packed, tags, points, arrived, pieces_out, tags_out,
-    pieces, tags_in, tags_s, send, buf,
-    w_send, w_recv, t_send, t_recv, l_sem, r_send, r_recv, c_send, c_recv, own,
+    packed, tags, points, head, wanted, arrived, pieces_out, tags_out, head_out, target,
+    pieces, tags_in, tags_s, send, buf, head_in, head_turned,
+    w_send, w_recv, t_send, t_recv, l_sem, r_send, r_recv, c_send, c_recv, h_send, h_recv, y_send, y_recv, own,
 ):
     me, feat = lax.axis_index("view"), lax.axis_index("feat")
     peers = packed.shape[0]
@@ -202,6 +202,22 @@
 
     lax.fori_loop(LAG, peers, both, 0)
     lax.fori_loop(peers - LAG + 1, peers, stage_b, 0)
+
+    def head_to(k):
+        return remote(head, head_in.at[feat], h_send.at[k - 1], h_recv.at[k - 1], me, (feat + k) % 4)
+
+    def wanted_to(k):
+        dst = (feat + k) % 4
+        return remote(wanted.at[dst], target.at[feat], y_send.at[k - 1], y_recv.at[k - 1], me, dst)
+
+    for k in (1, 3, 2):
+        head_to(k).start()
+    for k in (1, 3, 2):
+        wanted_to(k).start()
+    own_head = pltpu.make_async_copy(head, head_in.at[feat], own.at[3])
+    own_head.start()
+    own_wanted = pltpu.make_async_copy(wanted.at[feat], target.at[feat], own.at[4])
+    own_wanted.start()
     product(me)
     contrib_to(peer_at(me, 1, peers)).start()
     keep = pltpu.make_async_copy(pieces, pieces_out, own.at[0])
@@ -211,7 +227,26 @@
     own_contrib = pltpu.make_async_copy(send.at[me], arrived.at[me], own.at[2])
     own_contrib.start()
 
+    own_head.wait()
+    for k in (1, 2, 3):
+        head_to(k).wait_recv()
+
+    def turn(f, carry):
+        full = head_in[f].astype(jnp.float32)
+        mains = [full[:, 192 * c : 192 * c + 128] for c in range(4)]
+        tails = [full[:, 192 * c + 128 : 192 * c + 192] for c in range(4)]
+        head_turned[f] = jnp.concatenate(mains + tails, axis=1).astype(jnp.bfloat16)
+        return carry
+
+    lax.fori_loop(0, 4, turn, 0)
+    own_wanted.wait()
+    for k in (1, 2, 3):
+        head_to(k).wait_send()
+        wanted_to(k).wait_send()
+        wanted_to(k).wait_recv()
     others = pl.ds(0, peers - 1)
+    keep_head = pltpu.make_async_copy(head_turned, head_out, own.at[3])
+    keep_head.start()
     wait_bytes(packed.at[others], w_send)
     wait_bytes(tags.at[others], t_send)
     for k in range(3):
@@ -221,9 +256,10 @@
     keep.wait()
     keep_tags.wait()
     own_contrib.wait()
-
-
-def forward_exchange(packed, tags, points):
+    keep_head.wait()
+
+
+def forward_exchange(packed, tags, points, head, wanted):
     peers = packed.shape[0]
     whole = pl.BlockSpec(memory_space=pltpu.VMEM)
     dma = pltpu.SemaphoreType.DMA
@@ -234,21 +270,26 @@
             jax.ShapeDtypeStruct(slots, jnp.bfloat16),
             jax.ShapeDtypeStruct((4,) + packed.shape, jnp.bfloat16),
             jax.ShapeDtypeStruct(tags.shape, jnp.int32),
+            jax.ShapeDtypeStruct((4,) + head.shape, jnp.bfloat16),
+            jax.ShapeDtypeStruct(wanted.shape, jnp.bfloat16),
         ),
-        in_specs=[whole, whole, whole],
-        out_specs=(pl.BlockSpec(memory_space=pl.ANY),) * 3,
+        in_specs=[whole] * 5,
+        out_specs=(pl.BlockSpec(memory_space=pl.ANY),) * 5,
         scratch_shapes=[
             pltpu.VMEM((4,) + packed.shape, jnp.bfloat16),
             pltpu.VMEM(tags.shape, jnp.int32),
             pltpu.SMEM(tags.shape, jnp.int32),
             pltpu.VMEM(slots, jnp.bfloat16),
             pltpu.VMEM((CAP, SLOT, BLOCK), jnp.float32),
+            pltpu.VMEM((4,) + head.shape, jnp.bfloat16),
+            pltpu.VMEM((4,) + head.shape, jnp.bfloat16),
             dma, dma((peers,)), dma, dma((peers,)), dma((peers,)),
-            dma((3,)), dma((3, peers)), dma, dma, dma((3,)),
+            dma((3,)), dma((3, peers)), dma, dma,
+            dma((3,)), dma((3,)), dma((3,)), dma((3,)), dma((5,)),
         ],
         compiler_params=params(collective_id=0, has_side_effects=True),
         name="forward_exchange",
-    )(packed, tags, points)
+    )(packed, tags, points, head, wanted)
 
 
 def render_kernel(lines, source, line_of, arrived, out, acc):
@@ -301,81 +342,75 @@
     )(source, line_of, arrived)
 
 
-def widened(image, f, lines):
+def widened(image, f, start, lines):
     count = lines * LINE
     lane = lax.broadcasted_iota(jnp.int32, (count, BLOCK), 1)
-    pairs = image[f, 2].reshape(count, BLOCK)
-    zero = jnp.zeros_like(pairs)
-    upper = jnp.concatenate([image[f, 0].reshape(count, BLOCK), jnp.where(lane < 64, pairs, zero)], axis=1)
-    lower = jnp.concatenate([image[f, 1].reshape(count, BLOCK), jnp.where(lane < 64, zero, pairs)], axis=1)
+    parts = [image[f, j, pl.ds(start, lines)].reshape(count, BLOCK) for j in range(3)]
+    zero = jnp.zeros_like(parts[2])
+    upper = jnp.concatenate([parts[0], jnp.where(lane < 64, parts[2], zero)], axis=1)
+    lower = jnp.concatenate([parts[1], jnp.where(lane < 64, zero, parts[2])], axis=1)
     return jnp.concatenate([upper, lower], axis=0)
 
 
-def compare_kernel(rendered, head, target, grad_image, grad_proj):
-    count, width = 2 * LINE, target.shape[-1]
+def target_rows(target, start, lines):
+    count = lines * LINE
+    lane = lax.broadcasted_iota(jnp.int32, (count, BLOCK), 1)
+    part = [
+        [target[f, j, pl.ds(start, lines)].reshape(count, BLOCK).astype(jnp.float32) for j in range(3)] for f in range(4)
+    ]
+    halves = []
+    for half in range(2):
+        row = [part[f][half] for f in range(4)]
+        for f in (0, 2):
+            first, second = part[f][2], part[f + 1][2]
+            if half == 0:
+                second = pltpu.roll(second, 64, 1)
+            else:
+                first = pltpu.roll(first, 64, 1)
+            row.append(jnp.where(lane < 64, first, second))
+        halves.append(jnp.concatenate(row, axis=1))
+    return jnp.concatenate(halves, axis=0)
+
+
+def doubled(head, f):
+    full = head[f]
+    return jnp.concatenate([full, full[128:192]], axis=0)
+
+
+def compare_chunk(g, rendered, head, target, grad_image, grad_proj):
+    count, width = 2 * LINE, head.shape[-1]
     lane = lax.broadcasted_iota(jnp.int32, (count, BLOCK), 1)
     projected = jnp.zeros((2 * count, width), jnp.float32)
     for f in range(4):
-        projected += jnp.dot(widened(rendered, f, 2), head[f], preferred_element_type=jnp.float32)
+        projected += jnp.dot(widened(rendered, f, 2 * g, 2), doubled(head, f), preferred_element_type=jnp.float32)
     scale = jnp.sqrt(jnp.sum(projected * projected, axis=1, keepdims=True) / width + 1e-06)
     inverse = 1.0 / scale
     normed = projected * inverse
-    residual = normed - target[...].reshape(2 * count, width).astype(jnp.float32)
+    residual = normed - target_rows(target, 2 * g, 2)
     row_dot = jnp.sum(residual * normed, axis=1, keepdims=True) / width
     grad = ((residual - normed * row_dot) * inverse).astype(jnp.bfloat16)
-    grad_proj[...] = grad.reshape(grad_proj.shape)
+    grad_proj[:, pl.ds(2 * g, 2)] = grad.reshape(2, 2, LINE, width)
     for f in range(4):
-        image = lax.dot_general(grad, head[f], NT, preferred_element_type=jnp.float32)
+        image = lax.dot_general(grad, doubled(head, f), NT, preferred_element_type=jnp.float32)
         for half in range(2):
-            grad_image[f, half] = image[half * count : (half + 1) * count, 0:128].astype(jnp.bfloat16).reshape(2, LINE, BLOCK)
+            main = image[half * count : (half + 1) * count, 0:128]
+            grad_image[f, half, pl.ds(2 * g, 2)] = main.astype(jnp.bfloat16).reshape(2, LINE, BLOCK)
         pairs = jnp.where(lane < 64, image[0:count, 128:256], image[count : 2 * count, 128:256])
-        grad_image[f, 2] = pairs.astype(jnp.bfloat16).reshape(2, LINE, BLOCK)
-
-
-def compare(rendered, head, target):
-    width = target.shape[-1]
-    image = pl.BlockSpec((4, 3, 2, LINE, BLOCK), lambda i: (0, 0, i, 0, 0))
-    wide = pl.BlockSpec((2, 2, LINE, width), lambda i: (0, i, 0, 0))
-    return pl.pallas_call(
-        compare_kernel,
-        out_shape=(
-            jax.ShapeDtypeStruct(rendered.shape, jnp.bfloat16),
-            jax.ShapeDtypeStruct(target.shape, jnp.bfloat16),
-        ),
-        grid=(5,),
-        in_specs=[image, pl.BlockSpec(head.shape, lambda i: (0, 0, 0)), wide],
-        out_specs=(image, wide),
-        compiler_params=params(),
-        name="compare",
-    )(rendered, head, target)
-
-
-def head_kernel(rendered, grad_proj, out):
-    rows = widened(rendered, 0, 10)
-    for j in range(6):
-        grad = grad_proj[:, :, :, j * BLOCK : (j + 1) * BLOCK].reshape(rows.shape[0], BLOCK)
+        grad_image[f, 2, pl.ds(2 * g, 2)] = pairs.astype(jnp.bfloat16).reshape(2, LINE, BLOCK)
+
+
+def head_product(f, rendered, grad_proj, out):
+    rows = widened(rendered, f, 0, 10)
+    for j in range(3):
+        grad = grad_proj[:, :, :, j * 256 : (j + 1) * 256].reshape(rows.shape[0], 256)
         part = lax.dot_general(rows, grad, TN, preferred_element_type=jnp.float32)
-        out[0, j * 6 : j * 6 + 4] = part[0:128].reshape(4, 32, BLOCK)
-        out[0, j * 6 + 4 : j * 6 + 6] = (part[128:192] + part[192:256]).reshape(2, 32, BLOCK)
-
-
-def head_products(rendered, grad_proj):
-    rows = 4 * 10 * LINE * 256
-    return pl.pallas_call(
-        head_kernel,
-        out_shape=jax.ShapeDtypeStruct((4, 36, 32, BLOCK), jnp.float32),
-        grid=(4,),
-        in_specs=[
-            pl.BlockSpec((1,) + rendered.shape[1:], lambda i: (i, 0, 0, 0, 0)),
-            pl.BlockSpec(grad_proj.shape, lambda i: (0, 0, 0, 0)),
-        ],
-        out_specs=pl.BlockSpec((1, 36, 32, BLOCK), lambda i: (i, 0, 0, 0)),
-        compiler_params=params(),
-        name="head_products",
-    )(rendered, grad_proj)
-
-
-def line_slots_kernel(image, slots, buf):
+        for h in range(2):
+            base, cols = j * 12 + h * 6, part[:, h * 128 : (h + 1) * 128]
+            out[f, base : base + 4] = cols[0:128].reshape(4, 32, BLOCK)
+            out[f, base + 4 : base + 6] = (cols[128:192] + cols[192:256]).reshape(2, 32, BLOCK)
+
+
+def build_slots(image, slots, buf):
     lane = lax.broadcasted_iota(jnp.int32, (GRID, BLOCK), 1)
 
     def tail(at):
@@ -387,47 +422,96 @@
         own_half = (k // 10) % 2
         own_main = image[k // 20, own_half, k % 10, :, :].astype(jnp.float32)
         low_main = image[low // 20, low_half, low % 10, :, :].astype(jnp.float32)
-        buf[0:GRID, :] = own_main[0:GRID]
-        buf[GRID:ROWS, :] = low_main[0:GRID]
+        slot = k % 2
+        buf[slot, 0:GRID, :] = own_main[0:GRID]
+        buf[slot, GRID:ROWS, :] = low_main[0:GRID]
         own, lower = tail(k), tail(low)
         own = jnp.where(own_half == 0, own, pltpu.roll(own, 64, 1))
         lower = jnp.where(low_half == 1, lower, pltpu.roll(lower, 64, 1))
-        buf[ROWS : ROWS + GRID, :] = jnp.where(lane < 64, own, lower)
-        slots[k] = buf[...].astype(jnp.bfloat16)
+        buf[slot, ROWS : ROWS + GRID, :] = jnp.where(lane < 64, own, lower)
+        slots[k] = buf[slot].astype(jnp.bfloat16)
         return carry
 
     buf[...] = jnp.zeros_like(buf)
     lax.fori_loop(0, slots.shape[0], build, 0)
 
 
-def line_slots(image, lines):
-    whole = pl.BlockSpec(memory_space=pltpu.VMEM)
-    return pl.pallas_call(
-        line_slots_kernel,
-        out_shape=jax.ShapeDtypeStruct((lines, SLOT, BLOCK), jnp.bfloat16),
-        in_specs=[whole],
-        out_specs=whole,
-        scratch_shapes=[pltpu.VMEM((SLOT, BLOCK), jnp.float32)],
-        compiler_params=params(),
-        name="line_slots",
-    )(image)
-
-
 def backward_kernel(
-    source, line_of, slots, head_part, landed, head_out,
+    source, line_of, image, head, target, landed, head_out,
+    rendered, grad_image, grad_in, grad_proj, head_part, slots, buf,
     send, head_in, share, share_in, total, total_in,
+    p_send, p_recv, q_send, q_recv,
     g_send, g_recv, x_send, x_recv, a_send, a_recv, b_send, b_recv, own,
 ):
     me, feat = lax.axis_index("view"), lax.axis_index("feat")
     peers = send.shape[0]
     owners = share.shape[0]
+    own_image = pltpu.make_async_copy(image.at[feat], rendered.at[feat], own.at[0])
+    own_image.start()
     greet(me, feat, peers)
+
+    def image_to(k, g):
+        dst, chunk = (feat + k) % 4, pl.ds(2 * g, 2)
+        return remote(
+            image.at[dst, :, chunk], rendered.at[feat, :, chunk], p_send.at[k - 1, g], p_recv.at[k - 1, g], me, dst
+        )
+
+    def grads_back(k, g):
+        dst, chunk = (feat + k) % 4, pl.ds(2 * g, 2)
+        return remote(
+            grad_image.at[dst, :, chunk], grad_in.at[feat, :, chunk], q_send.at[k - 1, g], q_recv.at[k - 1, g], me, dst
+        )
+
+    def hand_out(g, carry):
+        for k in (1, 3, 2):
+            image_to(k, g).start()
+        return carry
+
+    lax.fori_loop(0, 5, hand_out, 0)
+    own_image.wait()
+
+    def chunk_step(g, carry):
+        for k in (1, 2, 3):
+            image_to(k, g).wait_recv()
+        compare_chunk(g, rendered, head, target, grad_image, grad_proj)
+
+        @pl.when(g > 0)
+        def _():
+            for k in (1, 3, 2):
+                grads_back(k, g - 1).start()
+
+        return carry
+
+    lax.fori_loop(0, 5, chunk_step, 0)
+    head_product(0, rendered, grad_proj, head_part)
+    for k in (1, 3, 2):
+        grads_back(k, 4).start()
+    own_back = pltpu.make_async_copy(grad_image.at[feat], grad_in.at[feat], own.at[0])
+    own_back.start()
+
+    def head_step(f, carry):
+        head_product(f, rendered, grad_proj, head_part)
+        return carry
+
+    lax.fori_loop(1, 4, head_step, 0)
+
+    def across(k):
+        return remote(head_part.at[(feat + k) % 4], head_in.at[k - 1], x_send.at[k - 1], x_recv.at[k - 1], me, (feat + k) % 4)
+
+    for k in (1, 3, 2):
+        across(k).start()
+
+    def returned(g, carry):
+        for k in (1, 2, 3):
+            grads_back(k, g).wait_recv()
+        return carry
+
+    lax.fori_loop(0, 5, returned, 0)
+    own_back.wait()
+    build_slots(grad_in, slots, buf)
 
     def grads_to(p):
         return remote(send.at[p], landed.at[me], g_send, g_recv, p, feat)
-
-    def across(k):
-        return remote(head_part.at[(feat + k) % 4], head_in.at[k - 1], x_send.at[k - 1], x_recv.at[k - 1], me, (feat + k) % 4)
 
     def pack(p):
         for s in range(CAP):
@@ -442,11 +526,8 @@
 
         return carry
 
-    for k in (1, 3, 2):
-        across(k).start()
-    middle = peers // 2
-    lax.fori_loop(1, middle, packed_to, 0)
-
+    early, late = peers * 3 // 8, peers * 3 // 4
+    lax.fori_loop(1, early, packed_to, 0)
     for k in (1, 2, 3):
         across(k).wait_recv()
 
@@ -456,7 +537,7 @@
         return carry
 
     lax.fori_loop(0, owners, add, 0)
-    lax.fori_loop(middle, middle + 4, packed_to, 0)
+    lax.fori_loop(early, early + 2, packed_to, 0)
 
     def share_to(p):
         return remote(share.at[p], share_in.at[me], a_send.at[p], a_recv, p, feat)
@@ -471,11 +552,7 @@
         return carry
 
     lax.fori_loop(1, peers, give, 0)
-    lax.fori_loop(middle + 4, peers, packed_to, 0)
-    pack(me)
-    grads_to(peer_at(me, peers - 1, peers)).start()
-    own_grads = pltpu.make_async_copy(send.at[me], landed.at[me], own.at[0])
-    own_grads.start()
+    lax.fori_loop(early + 2, late, packed_to, 0)
     others = pl.ds(0, peers - 1)
 
     def total_to(p, at):
@@ -502,6 +579,15 @@
             return carry
 
         lax.fori_loop(1, peers, tell, 0)
+
+    lax.fori_loop(late, peers, packed_to, 0)
+    pack(me)
+    grads_to(peer_at(me, peers - 1, peers)).start()
+    own_grads = pltpu.make_async_copy(send.at[me], landed.at[me], own.at[0])
+    own_grads.start()
+
+    @pl.when(me < owners)
+    def _():
         wait_bytes(share_in.at[others], b_send)
 
     def sent(i, carry):
@@ -517,6 +603,14 @@
     lax.fori_loop(1, peers, sent, 0)
     result = pltpu.make_async_copy(total_in, head_out, own.at[1])
     result.start()
+
+    def drain(g, carry):
+        for k in (1, 2, 3):
+            image_to(k, g).wait_send()
+            grads_back(k, g).wait_send()
+        return carry
+
+    lax.fori_loop(0, 5, drain, 0)
     for k in (1, 2, 3):
         across(k).wait_send()
     wait_bytes(send.at[others], g_send)
@@ -525,11 +619,10 @@
     result.wait()
 
 
-def backward_exchange(source, line_of, slots, head_part, peers):
+def backward_exchange(source, line_of, image, head, target, lines, peers):
     whole = pl.BlockSpec(memory_space=pltpu.VMEM)
     dma = pltpu.SemaphoreType.DMA
-    owners = head_part.shape[1]
-    tile = head_part.shape[2:]
+    owners, tile = 36, (32, BLOCK)
     shape = (peers, CAP * SLOT, BLOCK)
     return pl.pallas_call(
         backward_kernel,
@@ -537,23 +630,31 @@
             jax.ShapeDtypeStruct(shape, jnp.bfloat16),
             jax.ShapeDtypeStruct((owners,) + tile, jnp.bfloat16),
         ),
-        in_specs=[SMEM(), SMEM(), whole, whole],
+        in_specs=[SMEM(), SMEM(), whole, whole, whole],
         out_specs=(pl.BlockSpec(memory_space=pl.ANY),) * 2,
         scratch_shapes=[
+            pltpu.VMEM(image.shape, jnp.bfloat16),
+            pltpu.VMEM(image.shape, jnp.bfloat16),
+            pltpu.VMEM(image.shape, jnp.bfloat16),
+            pltpu.VMEM((2, 10, LINE, head.shape[-1]), jnp.bfloat16),
+            pltpu.VMEM((4, owners) + tile, jnp.float32),
+            pltpu.VMEM((lines, SLOT, BLOCK), jnp.bfloat16),
+            pltpu.VMEM((2, SLOT, BLOCK), jnp.float32),
             pltpu.VMEM(shape, jnp.bfloat16),
             pltpu.VMEM((3, owners) + tile, jnp.float32),
             pltpu.VMEM((owners,) + tile, jnp.bfloat16),
             pltpu.VMEM((peers,) + tile, jnp.bfloat16),
             pltpu.VMEM(tile, jnp.bfloat16),
             pltpu.VMEM((owners,) + tile, jnp.bfloat16),
+            dma((3, 5)), dma((3, 5)), dma((3, 5)), dma((3, 5)),
             dma, dma, dma((3,)), dma((3,)), dma((owners,)), dma, dma, dma((owners,)), dma((2,)),
         ],
         compiler_params=params(collective_id=1, has_side_effects=True),
         name="backward_exchange",
-    )(source, line_of, slots, head_part)
-
-
-def unsplat_kernel(ids, pieces, arrived, out, acc):
+    )(source, line_of, image, head, target)
+
+
+def unsplat_kernel(ids, pieces, arrived, out, acc, products):
     step = pl.program_id(0)
     lane = lax.broadcasted_iota(jnp.int32, (GRID, BLOCK), 1)
 
@@ -561,22 +662,28 @@
     def _():
         acc[...] = jnp.zeros_like(acc)
 
+    def product(i, s):
+        slot = arrived[i, pl.ds(s * SLOT, SLOT), :].astype(jnp.float32)
+        pair = slot[ROWS : ROWS + GRID]
+        rest = jnp.concatenate(
+            [jnp.where(lane < 64, pair, 0.0), jnp.where(lane < 64, 0.0, pair), jnp.zeros((6, BLOCK), jnp.float32)], axis=0
+        )
+        both = jnp.concatenate([slot[0:80], rest], axis=1).astype(jnp.bfloat16)
+        return lax.dot_general(both, slot_weights(pieces, i, s), TN, preferred_element_type=jnp.float32)
+
     def one(i, carry):
-        for s in range(CAP):
-            at = ids[(step * STEP + i) * CAP + s]
-            weights = slot_weights(pieces, i, s)
-            slot = arrived[i, pl.ds(s * SLOT, SLOT), :].astype(jnp.float32)
-            pair = slot[ROWS : ROWS + GRID]
-            rest = jnp.concatenate(
-                [jnp.where(lane < 64, pair, 0.0), jnp.where(lane < 64, 0.0, pair), jnp.zeros((6, BLOCK), jnp.float32)], axis=0
-            )
-            both = jnp.concatenate([slot[0:80], rest], axis=1).astype(jnp.bfloat16)
-            product = lax.dot_general(both, weights, TN, preferred_element_type=jnp.float32)
-            acc[at, 0:128, :] += product[0:128].astype(jnp.bfloat16).astype(jnp.float32)
-            acc[at, 128:192, :] += (product[128:192] + product[192:256]).astype(jnp.bfloat16).astype(jnp.float32)
-        return carry
-
-    lax.fori_loop(0, STEP, one, 0)
+        for n in range(2):
+            for s in range(CAP):
+                result = product(2 * i + n, s)
+                products[n * CAP + s, 0:128, :] = result[0:128]
+                products[n * CAP + s, 128:192, :] = result[128:192] + result[192:256]
+        for n in range(2):
+            for s in range(CAP):
+                at = ids[(step * STEP + 2 * i + n) * CAP + s]
+                acc[at] += products[n * CAP + s].astype(jnp.bfloat16).astype(jnp.float32)
+        return carry
+
+    lax.fori_loop(0, STEP // 2, one, 0)
 
     @pl.when(step == pl.num_programs(0) - 1)
     def _():
@@ -595,10 +702,16 @@
             pl.BlockSpec((STEP, CAP * SLOT, BLOCK), lambda i: (i, 0, 0)),
         ],
         out_specs=pl.BlockSpec(shape, lambda i: (0, 0, 0)),
-        scratch_shapes=[pltpu.VMEM(shape, jnp.float32)],
+        scratch_shapes=[pltpu.VMEM(shape, jnp.float32), pltpu.VMEM((2 * CAP,) + shape[1:], jnp.float32)],
         compiler_params=params(),
         name="unsplat",
     )(ids, pieces, arrived)
+
+
+def paired(rows):
+    rows = rows.reshape(4, 2, 10, LINE, 192)
+    tails = jnp.concatenate([rows[:, 0, :, :, 128:], rows[:, 1, :, :, 128:]], axis=-1)
+    return jnp.concatenate([rows[..., :128], tails[:, None]], axis=1)
 
 
 def per_device(points, head_weight, teacher, splat_weight, block_owner, block_local, block_row):
@@ -608,7 +721,6 @@
     views, visible = splat_weight.shape[:2]
     requests = views * visible
     lines = views * GRID
-    rows = 20 * LINE
 
     source, filled = slot_plan(block_owner.reshape(requests), peers, CAP)
     local = block_local.reshape(requests)
@@ -618,27 +730,21 @@
         jnp.pad(splat_weight, ((0, 0), (0, 0), (0, 4 * PIECE - ROWS), (0, 0))), feat * PIECE, PIECE, axis=2
     ).reshape(requests, PIECE, BLOCK)
     packed, tags = pack_weights(source, filled, local, mine, peers)
-
-    head = lax.all_gather(head_weight, "feat", axis=0)
-    head = jnp.concatenate([head, head[:, 128:192]], axis=1)
-    wanted = jnp.pad(
-        teacher.reshape(local_width, lines, GRID), ((0, 0), (0, 80 - lines), (0, LINE - GRID))
-    ).reshape(local_width, 4, rows)
-    target = lax.all_to_all(wanted.transpose(1, 0, 2), "feat", split_axis=0, concat_axis=0, tiled=True)
-    target = target.reshape(4 * local_width, rows).T.reshape(2, 10, LINE, 4 * local_width)
-
-    arrived, pieces, tags_in = forward_exchange(packed, tags, points)
+    wanted = paired(
+        jnp.pad(
+            teacher.transpose(1, 2, 0).reshape(lines, GRID, local_width), ((0, 80 - lines), (0, LINE - GRID), (0, 0))
+        )
+    )
+
+    arrived, pieces, tags_in, head, target = forward_exchange(packed, tags, points, head_weight, wanted)
     ids = tags_in[:, 0, :CAP].reshape(peers * CAP)
     image = render(source, line_of, arrived)
-    rendered = lax.all_to_all(image, "feat", split_axis=0, concat_axis=0, tiled=True)
-    grad_image, grad_proj = compare(rendered, head, target)
-    grad_rows = lax.all_to_all(grad_image, "feat", split_axis=0, concat_axis=0, tiled=True)
-    head_part = head_products(rendered, grad_proj)
-    slots = line_slots(grad_rows, lines)
-    landed, head_sum = backward_exchange(source, line_of, slots, head_part, peers)
+    landed, head_sum = backward_exchange(source, line_of, image, head, target, lines, peers)
     grad_points = unsplat(ids, pieces, landed, points.shape)
-    head_grad = head_sum.reshape(6, local_width, BLOCK).transpose(1, 0, 2).reshape(local_width, 6 * BLOCK)
-    return grad_points, head_grad.astype(jnp.float32) / (views * peers * GRID)
+    columns = head_sum.reshape(6, local_width, BLOCK).astype(jnp.float32)
+    tails = columns[4:].reshape(2, local_width, 2, 64).transpose(0, 2, 1, 3).reshape(4, local_width, 64)
+    head_grad = jnp.concatenate([columns[:4], tails], axis=2).transpose(1, 0, 2).reshape(local_width, 4 * 192)
+    return grad_points, head_grad / (views * peers * GRID)
 
 
 def solution(mesh):

time: 447 us -> 392 us (0.88)
  waiting for transfers between devices: 18.4 us -> 0 us
  starting transfers between devices: 15.8 us -> 0 us
  between operations: 14.1 us -> 0.84 us
  local copies, waits for them, and re-layouts: 16.2 us -> 9.94 us
    pallas_call x1, Pallas kernels: 151 us -> 185 us  [backward_exchange(): pl.pallas_call(backward_kernel, out_shape=(jax.ShapeDtypeStruct(shape, jn...]
    pallas_call x3 -> x0, Pallas kernels: 25.1 us -> none  [the longest x1 9.48 us: line_slots(): pl.pallas_call(line_slots_kernel, out_shape=jax.ShapeDtypeStruct((lines,...]
    all_to_all x3 -> x0, waiting for transfers between devices: 17.8 us -> none  [the longest x1 10.3 us: per_device(): lax.all_to_all(image, 'feat', split_axis=0, concat_axis=0, tiled=True)]
    all_to_all x3 -> x0, starting transfers between devices: 15.8 us -> none  [the longest x1 5.89 us: per_device(): lax.all_to_all(wanted.transpose(1, 0, 2), 'feat', split_axis=0, concat_ax...]
    pallas_call x1, Pallas kernels: 20.3 us -> 14.1 us  [unsplat(): pl.pallas_call(unsplat_kernel, out_shape=jax.ShapeDtypeStruct(shape, jnp....]
    unnamed x15 -> x13, local copies, waits for them, and re-layouts: 6.04 us -> 0.12 us
  transfers between devices with their start and end apart: 4 -> 0, of which waited for: 2 -> 0; matrix products, arithmetic and copies ran while one was open for 4% -> 0% of each run, Pallas kernels for 41% -> 0%
where the time goes in v3:
time: 392 us
  Pallas kernels  377 us (96%)
  local copies, waits for them, and re-layouts  9.94 us (3%)
  other arithmetic  4.23 us (1%)
    pallas_call x1, Pallas kernels, backward_exchange(): pl.pallas_call(backward_kernel, out_shape=(jax.ShapeDtypeStruct(shape, jn...  185 us
    pallas_call x1, Pallas kernels, forward_exchange(): pl.pallas_call(forward_kernel, out_shape=(jax.ShapeDtypeStruct(slots, jnp...  163 us
    pallas_call x1, Pallas kernels, unsplat(): pl.pallas_call(unsplat_kernel, out_shape=jax.ShapeDtypeStruct(shape, jnp....  14.1 us
    pallas_call x1, Pallas kernels, render(): pl.pallas_call(functools.partial(render_kernel, 80), out_shape=jax.ShapeD...  10.4 us

profile of v3, /device:TPU:2, one launch (start us, length us, event | category | flops | bytes accessed | tf_op | source)
XLA Modules:
  0.0 392.1 jit_solution(13482862814207109555)
XLA Ops:
  0.6 1.4 pad_dynamic-slice_fusion
  2.0 0.0 copy-start.3
  2.0 0.0 copy-start.5
  2.0 0.0 copy-start.1
  2.0 1.4 copy.20
  3.4 0.0 copy-done.3
  3.4 0.1 copy.19
  3.5 0.1 reshape.47
  3.6 0.2 convert_reduce_fusion
  3.8 0.7 select_reduce_fusion.source
  4.5 0.1 fusion.1
  4.6 0.6 convert_element_type.17.filled
  5.2 0.0 copy-done.5
  5.2 0.6 reshape.48.local
  5.8 4.5 %pack_weights.1 = (bf16[64,72,128]{2,1,0:T(8,128)(2,1)}, s32[64,1,128]{2,1,0:T(1,128)}) custom-call(s32[192]{0:T(256)} %select_reduce_fusion.source, s32[192]{0:T(256)} %convert_element_type.17.filled, s32[128]{0:T(128)} %reshape.48.local, bf16[128,24,128]{2,1,0:T(8,128)(2,1)} %bitcast.20), custom_call_target="tpu_custom_call" | custom-call | tf_op jit(solution)/shard_map/pack_weights/pallas_call | solution.py:91
  10.3 0.0 copy-done.1
  10.3 1.8 copy.21
  12.1 0.7 reshape.50
  12.8 0.3 pad.9
  13.1 0.1 slice_bitcast_fusion.1
  13.2 0.2 maximum_bitcast_fusion
  13.5 0.1 slice.35
  13.6 1.1 pad_maximum_fusion.wanted
  14.8 0.0 copy-start.4
  14.8 163.0 %forward_exchange.1 = (bf16[64,336,128]{2,1,0:T(8,128)(2,1)}, bf16[4,64,72,128]{3,2,1,0:T(8,128)(2,1)}, s32[64,1,128]{2,1,0:T(1,128)}, bf16[4,192,768]{2,1,0:T(8,128)(2,1)}, bf16[4,3,10,40,128]{4,3,2,1,0:T(8,128)(2,1)}) custom-call(bf16[64,72,128]{2,1,0:T(8,128)(2,1)} %get-tuple-element.11.packed, s32[64,1,128]{2,1,0:T(1,128)} %get-tuple-element.12.tags, ...), custom_call_target="tpu_custom_call" | custom-call | tf_op jit(solution)/shard_map/forward_exchange/pallas_call | solution.py:267
  177.8 0.0 copy-done.4
  177.8 0.1 broadcast_add_fusion
  177.9 0.6 reshape.52.line_of
  178.5 10.4 %render.1.image = bf16[4,3,10,40,128]{4,3,2,1,0:T(8,128)(2,1)} custom-call(s32[192]{0:T(256)} %select_reduce_fusion.source, s32[128]{0:T(128)} %reshape.52.line_of, bf16[64,336,128]{2,1,0:T(8,128)(2,1)} %get-tuple-element.15.arrived), custom_call_target="tpu_custom_call" | custom-call | tf_op jit(solution)/shard_map/render/pallas_call | solution.py:333
  188.9 185.1 %backward_exchange.1 = (bf16[64,336,128]{2,1,0:T(8,128)(2,1)}, bf16[36,32,128]{2,1,0:T(8,128)(2,1)}) custom-call(s32[192]{0:T(256)} %select_reduce_fusion.source, s32[128]{0:T(128)} %reshape.52.line_of, bf16[4,3,10,40,128]{4,3,2,1,0:T(8,128)(2,1)} %render.1.image, bf16[4,192,768]{2,1,0:T(8,128)(2,1)} %get-tuple-element.16.head, ...), custom_call_target="tpu_custom_call" | custom-call | tf_op jit(solution)/shard_map/backward_exchange/pallas_call | solution.py:627
  373.9 0.0 copy-start
  373.9 1.1 convert_element_type.18
  375.0 0.1 fusion.3
  375.2 0.0 copy-done
  375.2 0.1 fusion
  375.3 0.0 copy-start.2
  375.3 0.5 copy.24
  375.8 1.3 div.13
  377.1 0.0 copy-done.2
  377.2 0.1 slice_reduce_fusion
  377.2 0.7 reshape_squeeze.3.ids
  378.0 14.1 %unsplat.1 = bf16[64,192,128]{2,1,0:T(8,128)(2,1)} custom-call(s32[192]{0:T(256)} %reshape_squeeze.3.ids, bf16[4,64,72,128]{3,2,1,0:T(8,128)(2,1)} %get-tuple-element.14.pieces, bf16[64,336,128]{2,1,0:T(8,128)(2,1)} %get-tuple-element.18.arrived), custom_call_target="tpu_custom_call" | custom-call | tf_op jit(solution)/shard_map/unsplat/pallas_call | solution.py:695
  (4 shorter events, 0.1 us)
Async XLA Ops:
  2.0 1.4 copy-start.3
  2.0 3.2 copy-start.5
  2.0 8.3 %copy-start.1 = (bf16[192,2,1369]{2,1,0:T(2,128)(2,1)S(1)}, bf16[192,2,1369]{2,1,0:T(2,128)(2,1)}, u32[]{:S(2)}) copy-start(bf16[192,2,1369]{2,1,0:T(2,128)(2,1)} %param.9) | copy-start | bytes 3154180
  14.8 163.1 %copy-start.4 = (s32[2,64]{1,0:T(2,128)S(1)}, s32[2,64]{1,0:T(2,128)}, u32[]{:S(2)}) copy-start(s32[2,64]{1,0:T(2,128)} %param.13) | copy-start | bytes 1540
  373.9 1.3 copy-start
  375.3 1.8 copy-start.2

commit v4 on v3

v4 whole, which is shorter than its diff:
```python
import functools

import jax
import jax.numpy as jnp
from jax import lax
from jax.experimental import pallas as pl
from jax.experimental.pallas import tpu as pltpu
from jax.sharding import PartitionSpec as P

GRID = 37
BAND = 2
BLOCK = 128
CAP = 3
ROWS = BAND * GRID
PIECE = 56
FORMS = 192
SLOT = 112
LINE = 40
STEP = 8
PLANE = 8
PAIRS = 40
STRIDE = 27
LAG = 12
MESH = pl.DeviceIdType.MESH
SMEM = functools.partial(pl.BlockSpec, memory_space=pltpu.SMEM)
NT = (((1,), (1,)), ((), ()))
TN = (((0,), (0,)), ((), ()))
VMEM_LIMIT = 60 * 1024 * 1024


def params(**kw):
    return pltpu.CompilerParams(vmem_limit_bytes=VMEM_LIMIT, **kw)


def slot_plan(owners, peer_count, capacity):
    total_requests = owners.shape[0]
    positions = jnp.arange(total_requests, dtype=jnp.int32)
    earlier = (owners[:, None] == owners[None, :]) & (positions[None, :] < positions[:, None])
    slot_rank = jnp.sum(earlier.astype(jnp.int32), axis=1)
    target = owners * capacity + slot_rank
    slot_ids = jnp.arange(peer_count * capacity, dtype=jnp.int32)
    matches = target[None, :] == slot_ids[:, None]
    return jnp.sum(jnp.where(matches, positions[None, :] + 1, 0), axis=1) - 1


def entry_of(source, t):
    return jnp.maximum(source[t], 0)


def line_at(rows, entry):
    view = entry // rows.shape[1]
    return rows[view, entry % rows.shape[1]] + view * GRID


def peer_at(me, i, peers):
    return (me + i * STRIDE) % peers


def greet(me, feat, peers):
    barrier = pltpu.get_barrier_semaphore()

    def hello(i, carry):
        pl.semaphore_signal(barrier, inc=1, device_id=(peer_at(me, i, peers), feat), device_id_type=MESH)
        return carry

    lax.fori_loop(1, peers, hello, 0)
    for k in range(1, 4):
        pl.semaphore_signal(barrier, inc=1, device_id=(me, (feat + k) % 4), device_id_type=MESH)


def remote(src, dst, send, recv, view, feat):
    return pltpu.make_async_remote_copy(
        src_ref=src, dst_ref=dst, send_sem=send, recv_sem=recv, device_id=(view, feat), device_id_type=MESH
    )


def wait_bytes(ref, sem):
    pltpu.make_async_copy(ref, ref, sem).wait()


def cut_lines(teacher, lines, wanted):
    patches = teacher.shape[1]
    whole = patches // 32
    for v in range(teacher.shape[0]):

        def widen(t, carry):
            at = pl.ds(pl.multiple_of(32 * t, 32), 32)
            lines[v, at, :] = teacher[v, at, :].astype(jnp.float32)
            return carry

        lax.fori_loop(0, whole, widen, 0)
        lines[v, 32 * whole : patches, :] = teacher[v, 32 * whole : patches, :].astype(jnp.float32)

    def line(n):
        v, r = n // GRID, n % GRID
        if v >= teacher.shape[0]:
            return jnp.zeros((LINE, 192), jnp.float32)
        return jnp.concatenate([lines[v, r * GRID : (r + 1) * GRID, :], jnp.zeros((LINE - GRID, 192), jnp.float32)], axis=0)

    for f in range(4):
        for m in range(10):
            first, second = line(20 * f + m), line(20 * f + 10 + m)
            wanted[f, 0, m] = first[:, 0:128].astype(jnp.bfloat16)
            wanted[f, 1, m] = second[:, 0:128].astype(jnp.bfloat16)
            wanted[f, 2, m] = jnp.concatenate([first[:, 128:192], second[:, 128:192]], axis=1).astype(jnp.bfloat16)


def forward_kernel(
    source, local, rows, weights, points_far, head_far, teacher_far, arrived, forms_out, tags_out, head_out, target, tables_in,
    packed, tags, tables, pieces, tags_in, tags_s, send, buf, joined, forms, form, head_in, head_turned, points, head, teacher, lines, wanted,
    w_send, w_recv, t_send, t_recv, l_sem, r_send, r_recv, c_send, c_recv, h_send, h_recv, y_send, y_recv, k_send, k_recv, own, load,
):
    me, feat = lax.axis_index("view"), lax.axis_index("feat")
    loads = [
        pltpu.make_async_copy(src, dst, load.at[n])
        for n, (src, dst) in enumerate(((points_far, points), (head_far, head), (teacher_far, teacher)))
    ]
    for one in loads:
        one.start()
    peers = packed.shape[0]
    lane = lax.broadcasted_iota(jnp.int32, (GRID, BLOCK), 1)
    row = lax.broadcasted_iota(jnp.int32, (1, BLOCK), 1)
    visible = local.shape[1]
    greet(me, feat, peers)

    def pack(p):
        tag = jnp.zeros((1, BLOCK), jnp.int32)
        for s in range(CAP):
            entry = entry_of(source, p * CAP + s)
            joined[s * ROWS : (s + 1) * ROWS, :] = jnp.where(
                source[p * CAP + s] >= 0, weights[entry].astype(jnp.float32), 0.0
            )
            tag = jnp.where(row == s, local[entry // visible, entry % visible], tag)
        packed[p] = joined[pl.ds(pl.multiple_of(feat * PIECE, 8), PIECE), :].astype(jnp.bfloat16)
        tags[p] = tag

    joined[...] = jnp.zeros_like(joined)
    form[...] = jnp.zeros_like(form)
    inside = lax.broadcasted_iota(jnp.int32, (80, BLOCK), 0) < ROWS
    pack(me)
    pack(peer_at(me, 1, peers))
    pl.semaphore_wait(pltpu.get_barrier_semaphore(), peers + 2)
    own_piece = pltpu.make_async_copy(packed.at[me], pieces.at[feat, me], own.at[0])
    own_piece.start()
    own_tag = pltpu.make_async_copy(tags.at[me], tags_in.at[me], own.at[1])
    own_tag.start()

    def weights_to(p, at):
        return remote(packed.at[p], pieces.at[feat, at], w_send, w_recv.at[at], p, feat)

    def tags_to(p, at):
        return remote(tags.at[p], tags_in.at[at], t_send, t_recv.at[at], p, feat)

    def relay(q, k):
        return remote(
            pieces.at[feat, q], pieces.at[feat, q], r_send.at[k - 1], r_recv.at[k - 1, q], me, (feat + k) % 4
        )

    def relayed(q, k):
        came = (feat + 4 - k) % 4
        return remote(pieces.at[came, q], pieces.at[came, q], r_send.at[k - 1], r_recv.at[k - 1, q], me, came)

    def tag_copy(q):
        return pltpu.make_async_copy(tags_in.at[q], tags_s.at[q], l_sem.at[q])

    def contrib_to(q):
        return remote(send.at[q], arrived.at[me], c_send, c_recv, q, feat)

    def give(p):
        tags_to(p, me).start()
        weights_to(p, me).start()

    def first(i, carry):
        pack(peer_at(me, i, peers))
        give(peer_at(me, i - 1, peers))
        return carry

    lax.fori_loop(2, peers, first, 0)
    planes = peers // PLANE
    level, place = me // PLANE, me % PLANE

    def fill(n, carry):
        def entry(t, table):
            line = line_at(rows, entry_of(source, n * PLANE * CAP + t))
            after = line + 1
            table = jnp.where(row == t, (line // 2) % 5 * 8 + line // 10, table)
            return jnp.where(row == t + PLANE * CAP, (after // 2) % 5 * 8 + after // 10, table)

        tables[n] = lax.fori_loop(0, PLANE * CAP, entry, jnp.zeros((1, BLOCK), jnp.int32))
        return carry

    lax.fori_loop(0, planes, fill, 0)
    give(peer_at(me, peers - 1, peers))

    def pass_on(q):
        for k in (1, 3, 2):
            relay(q, k).start()
        tag_copy(q).start()

    def stage_a(i, carry):
        q = peer_at(me, peers - i, peers)
        tags_to(q, q).wait_recv()
        weights_to(q, q).wait_recv()
        pass_on(q)
        return carry

    def product(q):
        for k in (1, 2, 3):
            relayed(q, k).wait_recv()
        tag_copy(q).wait()
        full = jnp.concatenate([pieces[f, q].astype(jnp.float32) for f in range(4)], axis=0)
        full = jnp.concatenate([full, jnp.zeros((8, BLOCK), jnp.float32)], axis=0)
        for s in range(CAP):
            rows_s = jnp.where(inside, full[s * ROWS : s * ROWS + 80], 0.0)
            form[s, GRID : GRID + ROWS, :] = rows_s[0:ROWS]
            form[s, SLOT : SLOT + GRID, :] = rows_s[0:GRID]
            form[s, SLOT + LINE : SLOT + LINE + GRID, :] = rows_s[GRID:ROWS]
            forms[q, pl.ds(s * FORMS, FORMS), :] = form[s].astype(jnp.bfloat16)
            block = points[tags_s[q, 0, s]]
            wide = jnp.concatenate([block, block[128:192]], axis=0)
            result = lax.dot_general(rows_s.astype(jnp.bfloat16), wide, NT, preferred_element_type=jnp.float32)
            rest = result[:, 128:256]
            buf[s, 0:80, :] = result[:, 0:128]
            buf[s, ROWS : ROWS + GRID, :] = jnp.where(lane < 64, rest[0:GRID], rest[GRID:ROWS])
            buf[s, SLOT - 1 : SLOT, :] = jnp.zeros((1, BLOCK), jnp.float32)
            send[q, pl.ds(s * SLOT, SLOT), :] = buf[s].astype(jnp.bfloat16)

    def stage_b(i, carry):
        product(peer_at(me, peers - i, peers))

        @pl.when(i > 1)
        def _():
            contrib_to(peer_at(me, peers - i + 1, peers)).start()

        return carry

    for one in loads:
        one.wait()
    own_piece.wait()
    own_tag.wait()
    pass_on(me)
    lax.fori_loop(1, LAG, stage_a, 0)

    def both(i, carry):
        stage_a(i, carry)
        return stage_b(i - LAG + 1, carry)

    lax.fori_loop(LAG, peers, both, 0)
    lax.fori_loop(peers - LAG + 1, peers, stage_b, 0)

    def head_to(k):
        return remote(head, head_in.at[feat], h_send.at[k - 1], h_recv.at[k - 1], me, (feat + k) % 4)

    def wanted_to(k):
        dst = (feat + k) % 4
        return remote(wanted.at[dst], target.at[feat], y_send.at[k - 1], y_recv.at[k - 1], me, dst)

    cut_lines(teacher, lines, wanted)

    def table_to(i):
        there = (level + i) % planes
        return remote(
            tables.at[there], tables_in.at[level], k_send.at[i - 1], k_recv.at[i - 1], there * PLANE + place, feat
        )

    for i in range(1, planes):
        table_to(i).start()
    own_table = pltpu.make_async_copy(tables.at[level], tables_in.at[level], own.at[5])
    own_table.start()
    for k in (1, 3, 2):
        head_to(k).start()
    for k in (1, 3, 2):
        wanted_to(k).start()
    own_head = pltpu.make_async_copy(head, head_in.at[feat], own.at[3])
    own_head.start()
    own_wanted = pltpu.make_async_copy(wanted.at[feat], target.at[feat], own.at[4])
    own_wanted.start()
    product(me)
    contrib_to(peer_at(me, 1, peers)).start()
    keep = pltpu.make_async_copy(forms, forms_out, own.at[0])
    keep.start()
    keep_tags = pltpu.make_async_copy(tags_in, tags_out, own.at[1])
    keep_tags.start()
    own_contrib = pltpu.make_async_copy(send.at[me], arrived.at[me], own.at[2])
    own_contrib.start()

    own_head.wait()
    for k in (1, 2, 3):
        head_to(k).wait_recv()

    def turn(f, carry):
        full = head_in[f].astype(jnp.float32)
        mains = [full[:, 192 * c : 192 * c + 128] for c in range(4)]
        tails = [full[:, 192 * c + 128 : 192 * c + 192] for c in range(4)]
        turned = jnp.concatenate(mains + tails, axis=1).astype(jnp.bfloat16)
        head_turned[f] = jnp.concatenate([turned, turned[128:192]], axis=0)
        return carry

    lax.fori_loop(0, 4, turn, 0)
    own_wanted.wait()
    own_table.wait()
    for i in range(1, planes):
        table_to(i).wait_send()
        table_to(i).wait_recv()
    for k in (1, 2, 3):
        head_to(k).wait_send()
        wanted_to(k).wait_send()
        wanted_to(k).wait_recv()
    others = pl.ds(0, peers - 1)
    keep_head = pltpu.make_async_copy(head_turned, head_out, own.at[3])
    keep_head.start()
    wait_bytes(packed.at[others], w_send)
    wait_bytes(tags.at[others], t_send)
    for k in range(3):
        wait_bytes(packed, r_send.at[k])
    wait_bytes(send.at[others], c_send)
    wait_bytes(send.at[others], c_recv)
    keep.wait()
    keep_tags.wait()
    own_contrib.wait()
    keep_head.wait()


def forward_exchange(source, local, rows, weights, points, head, teacher, peers):
    whole = pl.BlockSpec(memory_space=pltpu.VMEM)
    dma = pltpu.SemaphoreType.DMA
    slots, wanted = (peers, CAP * SLOT, BLOCK), (4, 3, 10, LINE, BLOCK)
    forms, doubled = (peers, CAP * FORMS, BLOCK), (4, 256, head.shape[1])
    packed, tags, tables = (peers, PIECE, BLOCK), (peers, 1, BLOCK), (peers // PLANE, 1, BLOCK)
    return pl.pallas_call(
        forward_kernel,
        out_shape=(
            jax.ShapeDtypeStruct(slots, jnp.bfloat16),
            jax.ShapeDtypeStruct(forms, jnp.bfloat16),
            jax.ShapeDtypeStruct(tags, jnp.int32),
            jax.ShapeDtypeStruct(doubled, jnp.bfloat16),
            jax.ShapeDtypeStruct(wanted, jnp.bfloat16),
            jax.ShapeDtypeStruct(tables, jnp.int32),
        ),
        in_specs=[SMEM()] * 3 + [whole] + [pl.BlockSpec(memory_space=pl.ANY)] * 3,
        out_specs=(pl.BlockSpec(memory_space=pl.ANY),) * 6,
        scratch_shapes=[
            pltpu.VMEM(packed, jnp.bfloat16),
            pltpu.VMEM(tags, jnp.int32),
            pltpu.VMEM(tables, jnp.int32),
            pltpu.VMEM((4,) + packed, jnp.bfloat16),
            pltpu.VMEM(tags, jnp.int32),
            pltpu.SMEM(tags, jnp.int32),
            pltpu.VMEM(slots, jnp.bfloat16),
            pltpu.VMEM((CAP, SLOT, BLOCK), jnp.float32),
            pltpu.VMEM((4 * PIECE, BLOCK), jnp.float32),
            pltpu.VMEM(forms, jnp.bfloat16),
            pltpu.VMEM((CAP, FORMS, BLOCK), jnp.float32),
            pltpu.VMEM((4,) + head.shape, jnp.bfloat16),
            pltpu.VMEM(doubled, jnp.bfloat16),
            pltpu.VMEM(points.shape, jnp.bfloat16),
            pltpu.VMEM(head.shape, jnp.bfloat16),
            pltpu.VMEM(teacher.shape, jnp.bfloat16),
            pltpu.VMEM(teacher.shape, jnp.float32),
            pltpu.VMEM(wanted, jnp.bfloat16),
            dma, dma((peers,)), dma, dma((peers,)), dma((peers,)),
            dma((3,)), dma((3, peers)), dma, dma,
            dma((3,)), dma((3,)), dma((3,)), dma((3,)), dma((7,)), dma((7,)), dma((6,)), dma((3,)),
        ],
        compiler_params=params(collective_id=0, has_side_effects=True),
        name="forward_exchange",
    )(source, local, rows, weights, points, head, teacher)


def render_kernel(source, rows, arrived, out, acc):
    step = pl.program_id(0)
    lane = lax.broadcasted_iota(jnp.int32, (GRID, BLOCK), 1)

    @pl.when(step == 0)
    def _():
        acc[...] = jnp.zeros_like(acc)

    def one(i, carry):
        for s in range(CAP):
            at = line_at(rows, entry_of(source, (step * STEP + i) * CAP + s)) + 1
            acc[at] += arrived[i, pl.ds(s * SLOT, SLOT), :].astype(jnp.float32)
        return carry

    lax.fori_loop(0, STEP, one, 0, unroll=2)

    @pl.when(step == pl.num_programs(0) - 1)
    def _():
        out[...] = jnp.zeros_like(out)
        pairs = pl.ds(ROWS, GRID)

        def finish(k, carry):
            f, m = k // 10, k % 10
            for half in range(2):
                at = f * 20 + half * 10 + m
                out[f, half, m, 0:GRID, :] = (acc[at + 1, 0:GRID, :] + acc[at, GRID:ROWS, :]).astype(jnp.bfloat16)
            low, high = f * 20 + m, f * 20 + 10 + m
            turned = pltpu.roll(jnp.where(lane < 64, acc[high + 1, pairs, :], acc[low, pairs, :]), 64, 1)
            straight = jnp.where(lane < 64, acc[low + 1, pairs, :], acc[high, pairs, :])
            out[f, 2, m, 0:GRID, :] = (turned + straight).astype(jnp.bfloat16)
            return carry

        lax.fori_loop(0, 40, finish, 0, unroll=2)


def render(source, rows, arrived):
    peers = arrived.shape[0]
    shape = (4, 3, 10, LINE, BLOCK)
    return pl.pallas_call(
        render_kernel,
        out_shape=jax.ShapeDtypeStruct(shape, jnp.bfloat16),
        grid=(peers // STEP,),
        in_specs=[SMEM(), SMEM(), pl.BlockSpec((STEP, CAP * SLOT, BLOCK), lambda i: (i, 0, 0))],
        out_specs=pl.BlockSpec(shape, lambda i: (0, 0, 0, 0, 0)),
        scratch_shapes=[pltpu.VMEM((81, SLOT, BLOCK), jnp.float32)],
        compiler_params=params(),
        name="render",
    )(source, rows, arrived)


def widened(image, f, start, lines):
    count = lines * LINE
    lane = lax.broadcasted_iota(jnp.int32, (count, BLOCK), 1)
    parts = [image[f, j, pl.ds(start, lines)].reshape(count, BLOCK) for j in range(3)]
    zero = jnp.zeros_like(parts[2])
    upper = jnp.concatenate([parts[0], jnp.where(lane < 64, parts[2], zero)], axis=1)
    lower = jnp.concatenate([parts[1], jnp.where(lane < 64, zero, parts[2])], axis=1)
    return jnp.concatenate([upper, lower], axis=0)


def target_rows(target, start, lines):
    count = lines * LINE
    lane = lax.broadcasted_iota(jnp.int32, (count, BLOCK), 1)
    part = [
        [target[f, j, pl.ds(start, lines)].reshape(count, BLOCK).astype(jnp.float32) for j in range(3)] for f in range(4)
    ]
    halves = []
    for half in range(2):
        row = [part[f][half] for f in range(4)]
        for f in (0, 2):
            first, second = part[f][2], part[f + 1][2]
            if half == 0:
                second = pltpu.roll(second, 64, 1)
            else:
                first = pltpu.roll(first, 64, 1)
            row.append(jnp.where(lane < 64, first, second))
        halves.append(jnp.concatenate(row, axis=1))
    return jnp.concatenate(halves, axis=0)


def compare_chunk(g, rendered, head, target, grad_image, grad_proj):
    count, width = 2 * LINE, head.shape[-1]
    lane = lax.broadcasted_iota(jnp.int32, (count, BLOCK), 1)
    projected = jnp.zeros((2 * count, width), jnp.float32)
    for f in range(4):
        projected += jnp.dot(widened(rendered, f, 2 * g, 2), head[f], preferred_element_type=jnp.float32)
    scale = jnp.sqrt(jnp.sum(projected * projected, axis=1, keepdims=True) / width + 1e-06)
    inverse = 1.0 / scale
    normed = projected * inverse
    residual = normed - target_rows(target, 2 * g, 2)
    row_dot = jnp.sum(residual * normed, axis=1, keepdims=True) / width
    grad = ((residual - normed * row_dot) * inverse).astype(jnp.bfloat16)
    grad_proj[:, pl.ds(2 * g, 2)] = grad.reshape(2, 2, LINE, width)
    for f in range(4):
        image = lax.dot_general(grad, head[f], NT, preferred_element_type=jnp.float32)
        for half in range(2):
            main = image[half * count : (half + 1) * count, 0:128]
            grad_image[f, half, pl.ds(2 * g, 2)] = main.astype(jnp.bfloat16).reshape(2, LINE, BLOCK)
        pairs = jnp.where(lane < 64, image[0:count, 128:256], image[count : 2 * count, 128:256])
        grad_image[f, 2, pl.ds(2 * g, 2)] = pairs.astype(jnp.bfloat16).reshape(2, LINE, BLOCK)


def head_product(f, rendered, grad_proj, out):
    rows = widened(rendered, f, 0, 10)
    for j in range(3):
        grad = grad_proj[:, :, :, j * 256 : (j + 1) * 256].reshape(rows.shape[0], 256)
        part = lax.dot_general(rows, grad, TN, preferred_element_type=jnp.float32)
        for h in range(2):
            cols = part[:, h * 128 : (h + 1) * 128]
            full = jnp.concatenate([cols[0:128], cols[128:192] + cols[192:256]], axis=0)
            out[f, :, 2 * j + h] = full.reshape(PLANE, 24, BLOCK)


def build_pairs(g, image, pairs, buf):
    lane = lax.broadcasted_iota(jnp.int32, (GRID, BLOCK), 1)
    for seg in range(8):
        f, half, slot = seg // 2, seg % 2, seg % 2
        mains = [image[f, half, 2 * g + n].astype(jnp.float32)[0:GRID] for n in range(2)]
        tails = [image[f, 2, 2 * g + n].astype(jnp.float32)[0:GRID] for n in range(2)]
        tails[1 - half] = pltpu.roll(tails[1 - half], 64, 1)
        buf[slot, 0:GRID, :] = jnp.where(lane < 64, tails[0], tails[1])
        buf[slot, GRID:ROWS, :] = mains[0]
        buf[slot, ROWS : ROWS + GRID, :] = mains[1]
        pairs[8 * g + seg] = buf[slot].astype(jnp.bfloat16)


def backward_kernel(
    head_count, table, image, head_far, target_far, landed, head_out,
    rendered, grad_image, grad_in, grad_proj, head_part,
    own_pairs, up_1, up_2, up_3, down_1, down_2, down_3, far_pairs, buf,
    send, head_in, share, plane_in, level_sum, level_in, total, total_in, all_in, head_rows, head, target,
    p_send, p_recv, q_send, q_recv, z_send, z_recv,
    g_send, g_recv, x_send, x_recv, a_send, a_recv, c_send, c_recv, d_send, d_recv, e_send, e_recv, own, kept, load,
):
    me, feat = lax.axis_index("view"), lax.axis_index("feat")
    planes = level_in.shape[0] + 1
    held = ((own_pairs, up_1, up_2, up_3, far_pairs), (own_pairs, down_1, down_2, down_3, far_pairs))
    level, place = me // PLANE, me % PLANE
    lane = lax.broadcasted_iota(jnp.int32, (GRID, BLOCK), 1)
    own_image = pltpu.make_async_copy(image.at[feat], rendered.at[feat], own.at[0])
    own_image.start()
    loads = [
        pltpu.make_async_copy(src, dst, load.at[n])
        for n, (src, dst) in enumerate(((head_far, head), (target_far, target)))
    ]
    for one in loads:
        one.start()

    def at_level(i):
        return ((level + i) % planes) * PLANE + place

    def in_plane(i):
        return level * PLANE + (place + i) % PLANE

    barrier = pltpu.get_barrier_semaphore()
    for k in range(1, 4):
        pl.semaphore_signal(barrier, inc=1, device_id=(me, (feat + k) % 4), device_id_type=MESH)
    for i in range(1, planes):
        pl.semaphore_signal(barrier, inc=1, device_id=(at_level(i), feat), device_id_type=MESH)
    for i in range(1, PLANE):
        pl.semaphore_signal(barrier, inc=1, device_id=(in_plane(i), feat), device_id_type=MESH)
    pl.semaphore_wait(barrier, 3 + planes - 1 + PLANE - 1)

    def image_to(k, g):
        dst, chunk = (feat + k) % 4, pl.ds(2 * g, 2)
        return remote(
            image.at[dst, :, chunk], rendered.at[feat, :, chunk], p_send.at[k - 1, g], p_recv.at[k - 1, g], me, dst
        )

    def grads_back(k, g):
        dst, chunk = (feat + k) % 4, pl.ds(2 * g, 2)
        return remote(
            grad_image.at[dst, :, chunk], grad_in.at[feat, :, chunk], q_send.at[k - 1, g], q_recv.at[k - 1, g], me, dst
        )

    def own_back(g):
        chunk = pl.ds(2 * g, 2)
        return pltpu.make_async_copy(grad_image.at[feat, :, chunk], grad_in.at[feat, :, chunk], kept.at[g])

    def each_size(g, act):
        @pl.when(g < 2)
        def _():
            act(8)

        @pl.when(g >= 2)
        def _():
            act(7)

    def ring(way, hop, g, count):
        chunk = pl.ds(8 * g, count)
        src, dst = held[way][hop].at[chunk], held[way][hop + 1].at[chunk]
        return remote(src, dst, z_send.at[way, hop, g], z_recv.at[way, hop, g], at_level(planes + 1 - 2 * way), feat)

    def ring_send(way, hop, g):
        each_size(g, lambda count: ring(way, hop, g, count).start())

    def ring_wait(way, hop, g):
        each_size(g, lambda count: ring(way, hop, g, count).wait_recv())

    def ring_sent(way, hop, g):
        each_size(g, lambda count: ring(way, hop, g, count).wait_send())

    def hand_out(g, carry):
        for k in (1, 3, 2):
            image_to(k, g).start()
        return carry

    lax.fori_loop(0, 5, hand_out, 0)
    buf[...] = jnp.zeros_like(buf)
    own_image.wait()
    for one in loads:
        one.wait()

    def returned(g):
        own_back(g).wait()
        for k in (1, 2, 3):
            grads_back(k, g).wait_recv()
        build_pairs(g, grad_in, own_pairs, buf)
        ring_send(0, 0, g)
        ring_send(1, 0, g)

    def chunk_step(g, carry):
        for k in (1, 2, 3):
            image_to(k, g).wait_recv()
        compare_chunk(g, rendered, head, target, grad_image, grad_proj)
        own_back(g).start()
        for k in (1, 3, 2):
            grads_back(k, g).start()

        @pl.when(g > 0)
        def _():
            returned(g - 1)

        return carry

    lax.fori_loop(0, 5, chunk_step, 0)
    returned(4)

    def grads_to(origin, i):
        return remote(
            send.at[origin * PLANE + (place + i) % PLANE], landed.at[origin * PLANE + place], g_send, g_recv, in_plane(i), feat
        )

    def pack(origin, pairs, i):
        to = (place + i) % PLANE
        for s in range(CAP):
            first, second = table[origin, 0, to * CAP + s], table[origin, 0, PLANE * CAP + to * CAP + s]
            own_pair = pairs[first].astype(jnp.float32)
            next_pair = pairs[second].astype(jnp.float32)
            buf[s, 0:GRID, :] = pltpu.roll(jnp.where(lane < 64, next_pair[0:GRID], own_pair[0:GRID]), 64, 1)
            buf[s, GRID:ROWS, :] = own_pair[ROWS : ROWS + GRID]
            buf[s, ROWS : ROWS + GRID, :] = next_pair[GRID:ROWS]
            slot = jnp.where(first == second, own_pair, buf[s])
            send[origin * PLANE + to, pl.ds(s * SLOT, SLOT), :] = slot.astype(jnp.bfloat16)

    def deal(origins, start, stop):
        def one(i, carry):
            for origin, pairs in origins:
                pack(origin, pairs, i)

            @pl.when(i > 0)
            def _():
                for origin, _ in origins:
                    grads_to(origin, i).start()

            return carry

        lax.fori_loop(start, stop, one, 0)

    def both_at(d):
        return (((level + planes - d) % planes, held[0][d]), ((level + d) % planes, held[1][d]))

    def head_step(f, carry):
        head_product(f, rendered, grad_proj, head_part)
        return carry

    def across(k):
        return remote(head_part.at[(feat + k) % 4], head_in.at[k - 1], x_send.at[k - 1], x_recv.at[k - 1], me, (feat + k) % 4)

    def share_to(i):
        return remote(share.at[(place + i) % PLANE], plane_in.at[i - 1], a_send.at[i - 1], a_recv.at[i - 1], in_plane(i), feat)

    owners = total_in.shape[0]

    def level_to(i):
        there = (level + i) % planes
        return remote(level_sum.at[there], level_in.at[i - 1], c_send.at[i - 1], c_recv.at[i - 1], at_level(i), feat)

    def total_to(i, origin):
        return remote(total, total_in.at[origin], d_send.at[i - 1], d_recv.at[i - 1], at_level(i), feat)

    def all_to(i, origin):
        return remote(total_in, all_in.at[origin], e_send.at[i - 1], e_recv.at[i - 1], in_plane(i), feat)

    def came_down(g, d, last):
        up, down = g < 2, g >= 2
        ring_wait(0, d - 1, g)
        if last:
            pl.when(up)(lambda: ring_send(0, d, g))
        else:
            ring_send(0, d, g)
        ring_wait(1, d - 1, g)
        if last:
            pl.when(down)(lambda: ring_send(1, d, g))
        else:
            ring_send(1, d, g)

    def first_step(g, carry):
        came_down(g, 1, False)
        return carry

    deal(((level, own_pairs),), 0, PLANE)
    lax.fori_loop(0, 4, head_step, 0)
    for k in (1, 3, 2):
        across(k).start()
    lax.fori_loop(0, 5, first_step, 0)
    deal(both_at(1), 0, PLANE)

    for k in (1, 2, 3):
        across(k).wait_recv()

    def add(t, carry):
        share[t] = head_part[feat, t] + head_in[0, t] + head_in[1, t] + head_in[2, t]
        return carry

    lax.fori_loop(0, PLANE, add, 0)

    def second_step(g, carry):
        came_down(g, 2, False)
        return carry

    lax.fori_loop(0, 1, second_step, 0)
    for i in range(1, PLANE):
        share_to(i).start()
    lax.fori_loop(1, 5, second_step, 0)
    deal(both_at(2), 0, PLANE)

    for i in range(1, PLANE):
        share_to(i).wait_recv()
    value = share[place]
    for i in range(PLANE - 1):
        value += plane_in[i]
    level_sum[...] = value

    def third_step(g, carry):
        came_down(g, 3, True)
        return carry

    lax.fori_loop(0, 1, third_step, 0)
    for i in range(1, planes):
        pl.when((level + i) % planes < owners)(lambda i=i: level_to(i).start())
    lax.fori_loop(1, 5, third_step, 0)
    deal(both_at(3), 0, PLANE)

    @pl.when(level < owners)
    def _():
        for i in range(1, planes):
            came = remote(level_sum.at[level], level_in.at[i - 1], c_send.at[i - 1], c_recv.at[i - 1], at_level(i), feat)
            came.wait_recv()
        value = level_sum[level]
        for i in range(planes - 1):
            value += level_in[i]
        total[...] = value

    def fourth_step(g, carry):
        up, down = g < 2, g >= 2
        pl.when(up)(lambda: ring_wait(0, 3, g))
        pl.when(down)(lambda: ring_wait(1, 3, g))
        return carry

    lax.fori_loop(0, 1, fourth_step, 0)

    @pl.when(level < owners)
    def _():
        for i in range(1, planes):
            total_to(i, level).start()
        mine = pltpu.make_async_copy(total, total_in.at[level], own.at[1])
        mine.start()
        mine.wait()

    lax.fori_loop(1, 5, fourth_step, 0)
    deal((((level + 4) % planes, far_pairs),), 0, PLANE)

    def own_slots(origin):
        at = origin * PLANE + place
        return pltpu.make_async_copy(send.at[at], landed.at[at], kept.at[origin])

    for origin in range(planes):
        own_slots(origin).start()
    for i in range(1, planes):
        origin = (level + planes - i) % planes
        pl.when(origin < owners)(lambda i=i, origin=origin: total_to(i, origin).wait_recv())
    for i in range(1, PLANE):
        all_to(i, place).start()
    mine = pltpu.make_async_copy(total_in, all_in.at[place], own.at[1])
    mine.start()
    mine.wait()
    for i in range(1, PLANE):
        all_to(i, (place + PLANE - i) % PLANE).wait_recv()

    def arrange(u, carry):
        parts = []
        for f in range(4):
            tail = all_in[u, 4 + f // 2]
            parts += [all_in[u, f], tail[:, 64 * (f % 2) : 64 * (f % 2) + 64]]
        head_rows[pl.ds(pl.multiple_of(24 * u, 8), 24), :] = jnp.concatenate(parts, axis=1) / head_count
        return carry

    lax.fori_loop(0, PLANE, arrange, 0)

    def drain(g, carry):
        for k in (1, 2, 3):
            image_to(k, g).wait_send()
            grads_back(k, g).wait_send()
        for way in range(2):
            for hop in range(3):
                ring_sent(way, hop, g)
        pl.when(g < 2)(lambda: ring_sent(0, 3, g))
        pl.when(g >= 2)(lambda: ring_sent(1, 3, g))
        return carry

    lax.fori_loop(0, 5, drain, 0)
    for k in (1, 2, 3):
        across(k).wait_send()
    for i in range(1, PLANE):
        share_to(i).wait_send()
        all_to(i, place).wait_send()
    for i in range(1, planes):
        pl.when((level + i) % planes < owners)(lambda i=i: level_to(i).wait_send())
        pl.when(level < owners)(lambda i=i: total_to(i, level).wait_send())
    others = pl.ds(0, planes * (PLANE - 1))
    result = pltpu.make_async_copy(head_rows, head_out, own.at[1])
    result.start()
    wait_bytes(send.at[others], g_send)
    wait_bytes(send.at[others], g_recv)
    for origin in range(planes):
        own_slots(origin).wait()
    result.wait()


def backward_exchange(table, image, head, target, peers, head_count):
    whole = pl.BlockSpec(memory_space=pltpu.VMEM)
    dma = pltpu.SemaphoreType.DMA
    planes, owners, tile = peers // PLANE, 6, (24, BLOCK)
    shape = (peers, CAP * SLOT, BLOCK)
    share = (PLANE, owners) + tile
    return pl.pallas_call(
        functools.partial(backward_kernel, float(head_count)),
        out_shape=(
            jax.ShapeDtypeStruct(shape, jnp.bfloat16),
            jax.ShapeDtypeStruct((192, head.shape[-1]), jnp.float32),
        ),
        in_specs=[SMEM(), whole, pl.BlockSpec(memory_space=pl.ANY), pl.BlockSpec(memory_space=pl.ANY)],
        out_specs=(pl.BlockSpec(memory_space=pl.ANY),) * 2,
        scratch_shapes=[
            pltpu.VMEM(image.shape, jnp.bfloat16),
            pltpu.VMEM(image.shape, jnp.bfloat16),
            pltpu.VMEM(image.shape, jnp.bfloat16),
            pltpu.VMEM((2, 10, LINE, head.shape[-1]), jnp.bfloat16),
            pltpu.VMEM((4,) + share, jnp.float32),
            *[pltpu.VMEM((PAIRS, SLOT, BLOCK), jnp.bfloat16)] * planes,
            pltpu.VMEM((CAP, SLOT, BLOCK), jnp.float32),
            pltpu.VMEM(shape, jnp.bfloat16),
            pltpu.VMEM((3,) + share, jnp.float32),
            pltpu.VMEM(share, jnp.float32),
            pltpu.VMEM((PLANE - 1, owners) + tile, jnp.float32),
            pltpu.VMEM((owners,) + tile, jnp.float32),
            pltpu.VMEM((planes - 1,) + tile, jnp.float32),
            pltpu.VMEM(tile, jnp.float32),
            pltpu.VMEM((owners,) + tile, jnp.float32),
            pltpu.VMEM(share, jnp.float32),
            pltpu.VMEM((192, head.shape[-1]), jnp.float32),
            pltpu.VMEM(head.shape, jnp.bfloat16),
            pltpu.VMEM(target.shape, jnp.bfloat16),
            dma((3, 5)), dma((3, 5)), dma((3, 5)), dma((3, 5)), dma((2, 4, 5)), dma((2, 4, 5)),
            dma, dma, dma((3,)), dma((3,)), dma((7,)), dma((7,)), dma((7,)), dma((7,)),
            dma((7,)), dma((7,)), dma((7,)), dma((7,)), dma((2,)), dma((8,)), dma((2,)),
        ],
        compiler_params=params(collective_id=1, has_side_effects=True),
        name="backward_exchange",
    )(table, image, head, target)


def unsplat_kernel(tags, forms, arrived, out, acc, products):
    step = pl.program_id(0)

    @pl.when(step == 0)
    def _():
        acc[...] = jnp.zeros_like(acc)

    def product(i, s, at):
        slot, base = arrived[i, pl.ds(s * SLOT, SLOT), :], s * FORMS
        main = lax.dot_general(slot, forms[i, pl.ds(base, SLOT), :], TN, preferred_element_type=jnp.float32)
        both = [forms[i, pl.ds(base + SLOT + n * LINE, LINE), :] for n in range(2)]
        rest = lax.dot_general(slot[0:LINE], jnp.concatenate(both, axis=1), TN, preferred_element_type=jnp.float32)
        products[at, 0:128, :] = main.astype(jnp.bfloat16)
        products[at, 128:192, :] = (rest[0:64, 0:128] + rest[64:128, 128:256]).astype(jnp.bfloat16)

    def one(i, carry):
        for n in range(STEP):
            for s in range(CAP):
                product(n, s, n * CAP + s)
        for n in range(STEP):
            for s in range(CAP):
                acc[tags[step * STEP + n, 0, s]] += products[n * CAP + s].astype(jnp.float32)
        return carry

    lax.fori_loop(0, 1, one, 0)

    @pl.when(step == pl.num_programs(0) - 1)
    def _():
        out[...] = acc[...].astype(jnp.bfloat16)


def unsplat(tags, forms, arrived, shape):
    peers = arrived.shape[0]
    return pl.pallas_call(
        unsplat_kernel,
        out_shape=jax.ShapeDtypeStruct(shape, jnp.bfloat16),
        grid=(peers // STEP,),
        in_specs=[
            SMEM(),
            pl.BlockSpec((STEP, CAP * FORMS, BLOCK), lambda i: (i, 0, 0)),
            pl.BlockSpec((STEP, CAP * SLOT, BLOCK), lambda i: (i, 0, 0)),
        ],
        out_specs=pl.BlockSpec(shape, lambda i: (0, 0, 0)),
        scratch_shapes=[pltpu.VMEM(shape, jnp.float32), pltpu.VMEM((STEP * CAP,) + shape[1:], jnp.bfloat16)],
        compiler_params=params(),
        name="unsplat",
    )(tags, forms, arrived)


def per_device(points, head_weight, teacher, splat_weight, block_owner, block_local, block_row):
    peers = lax.axis_size("view")
    views, visible = splat_weight.shape[:2]
    requests = views * visible

    source = slot_plan(block_owner.reshape(requests), peers, CAP)
    weights = splat_weight.reshape(requests, ROWS, BLOCK)
    arrived, forms, tags, head, target, table = forward_exchange(
        source, block_local, block_row, weights, points, head_weight, teacher.transpose(1, 2, 0), peers
    )
    image = render(source, block_row, arrived)
    landed, head_grad = backward_exchange(table, image, head, target, peers, views * peers * GRID)
    return unsplat(tags, forms, landed, points.shape), head_grad


def solution(mesh):
    placed = (
        P("view", "feat", None),
        P("feat", None),
        P("feat", "view", None),
        P("view", None, None, None),
        P("view", None, None),
        P("view", None),
        P("view", None),
    )
    return jax.shard_map(
        per_device,
        mesh=mesh,
        in_specs=placed,
        out_specs=(P("view", "feat", None), P("feat", None)),
        check_vma=False,
    )
```

time: 392 us -> 320 us (0.82)
  Pallas kernels: 377 us -> 307 us
    pallas_call x3 -> x2, Pallas kernels: 200 us -> 135 us  [the longest x1 126 us: backward_exchange(): pl.pallas_call(functools.partial(backward_kernel, float(head_count)), out...]
    unnamed x13 -> x8, local copies, waits for them, and re-layouts: 0.12 us -> 8.56 us
    pallas_call x1, Pallas kernels: 163 us -> 158 us  [forward_exchange(): pl.pallas_call(forward_kernel, out_shape=(jax.ShapeDtypeStruct(slots, jnp...]
where the time goes in v4:
time: 320 us; the launch traced here: 317 us
  Pallas kernels  307 us (96%)
  local copies, waits for them, and re-layouts  8.67 us (3%)
    pallas_call x1, Pallas kernels, forward_exchange(): pl.pallas_call(forward_kernel, out_shape=(jax.ShapeDtypeStruct(slots, jnp...  158 us
    pallas_call x1, Pallas kernels, backward_exchange(): pl.pallas_call(functools.partial(backward_kernel, float(head_count)), out...  126 us
    pallas_call x1, Pallas kernels, unsplat(): pl.pallas_call(unsplat_kernel, out_shape=jax.ShapeDtypeStruct(shape, jnp....  12.9 us
    pallas_call x1, Pallas kernels, render(): pl.pallas_call(render_kernel, out_shape=jax.ShapeDtypeStruct(shape, jnp.b...  9.23 us
    unnamed x8, local copies, waits for them, and re-layouts  8.56 us

profile of v4, /device:TPU:2, one launch (start us, length us, event | category | flops | bytes accessed | tf_op | source)
XLA Modules:
  0.0 316.9 jit_solution(3932492000831409703)
XLA Ops:
  0.6 0.0 copy-start
  0.6 0.9 copy.15
  1.6 0.1 reshape.25
  1.7 0.2 convert_reduce_fusion
  1.9 0.1 select_reduce_fusion
  2.0 0.6 broadcast_add_fusion.source
  2.6 3.7 %copy.17 = bf16[192,2,1369]{0,2,1:T(8,128)(2,1)} copy(bf16[192,2,1369]{2,1,0:T(2,128)(2,1)} %param.9) | data formatting | bytes 2102784 | tf_op args[2]
  6.3 0.0 copy-done
  6.3 3.1 copy.16
  9.4 158.3 %forward_exchange.1 = (bf16[64,336,128]{2,1,0:T(8,128)(2,1)}, bf16[64,576,128]{2,1,0:T(8,128)(2,1)}, s32[64,1,128]{2,1,0:T(1,128)}, bf16[4,256,768]{2,1,0:T(8,12...) custom-call(s32[192]{0:T(256)} %broadcast_add_fusion.source, s32[2,64]{1,0:T(2,128)} %local.1, ...), custom_call_target="tpu_custom_call" | custom-call | tf_op jit(solution)/shard_map/forward_exchange/pallas_call | solution.py:330
  167.7 9.2 %render.1.image = bf16[4,3,10,40,128]{4,3,2,1,0:T(8,128)(2,1)} custom-call(s32[192]{0:T(256)} %broadcast_add_fusion.source, s32[2,64]{1,0:T(2,128)} %rows.3, bf16[64,336,128]{2,1,0:T(8,128)(2,1)} %get-tuple-element.13.arrived), custom_call_target="tpu_custom_call" | custom-call | tf_op jit(solution)/shard_map/render/pallas_call | solution.py:408
  176.9 126.2 %backward_exchange.1 = (bf16[64,336,128]{2,1,0:T(8,128)(2,1)}, f32[192,768]{1,0:T(8,128)}) custom-call(s32[8,1,128]{2,1,0:T(1,128)} %get-tuple-element.12.table, bf16[4,3,10,40,128]{4,3,2,1,0:T(8,128)(2,1)} %render.1.image, bf16[4,256,768]{2,1,0:T(8,128)(2,1)} %get-tuple-element.14.head_far, bf16[4,3,10,40,128]{4,3,2,1,0:T(8,128)(2,1)} %get-tuple-element.15.target_far), custom_call_target="tpu_custom_call" | custom-call | tf_op jit(solution)/shard_map/backward_exchange/pallas_call | solution.py:816
  303.1 0.0 copy-start.1
  303.1 12.9 %unsplat.1 = bf16[64,192,128]{2,1,0:T(8,128)(2,1)} custom-call(s32[64,1,128]{2,1,0:T(1,128)} %get-tuple-element.10.tags, bf16[64,576,128]{2,1,0:T(8,128)(2,1)} %get-tuple-element.11.forms, bf16[64,336,128]{2,1,0:T(8,128)(2,1)} %get-tuple-element.16.arrived), custom_call_target="tpu_custom_call" | custom-call | tf_op jit(solution)/shard_map/unsplat/pallas_call | solution.py:886
  316.0 0.0 copy-done.1
  316.0 0.8 copy.19
  (1 shorter events, 0.0 us)
Async XLA Ops:
  0.6 5.7 %copy-start = (bf16[2,64,74,128]{3,1,2,0:T(8,128)(2,1)S(1)}, bf16[2,64,74,128]{3,1,2,0:T(8,128)(2,1)}, u32[]{:S(2)}) copy-start(bf16[2,64,74,128]{3,1,2,0:T(8,128)(2,1)} %param.10) | copy-start | bytes 7274500
  303.1 12.9 %copy-start.1 = (f32[192,768]{1,0:T(8,128)S(1)}, f32[192,768]{1,0:T(8,128)}, u32[]{:S(2)}) copy-start(f32[192,768]{1,0:T(8,128)} %get-tuple-element.23) | copy-start | bytes 1769476
